TPU v7x, 32 devices: a whole 2x2x4 slice. The times are simulated.
32 devices in a mesh: groups: 2 (over y), row: 4 (over z), col: 4 (over x, core).
Axes of the slice: x: 2, y: 2, z: 4, core: 2. Of those that a mesh axis runs over, the one named last changes fastest.
Arguments:
- tokens: bfloat16 [128, 8192], P(('groups', 'row'), 'col'), parts along dimension 0, may hold values from -6 to 6
- gate_tiles: bfloat16 [256, 4, 12, 128, 256], P(('groups', 'row'), 'col'), parts along dimension 0, may hold values from -0.09375 to 0.09375
- gate_lists: int32 [256, 4, 12], P(('groups', 'row'), 'col'), parts along dimension 0, may hold values from 0 to 15, as said below
- gate_counts: int32 [256, 4], P(('groups', 'row'), 'col'), parts along dimension 0, may hold values from 4 to 12, as said below
- down_tiles: bfloat16 [128, 4, 24, 128, 128], P(('groups', 'row'), 'col'), parts along dimension 0, may hold values from -0.0625 to 0.0625
- down_lists: int32 [128, 4, 24], P(('groups', 'row'), 'col'), parts along dimension 0, may hold values from 0 to 31, as said below
- down_counts: int32 [128, 4], P(('groups', 'row'), 'col'), parts along dimension 0, may hold values from 8 to 24, as said below
Outputs:
- ffn_out: bfloat16 [128, 8192], P(('groups', 'col'), 'row'), parts along dimension 0
There are 2 independent parts, one for each index of `groups`. A program takes and returns all parts, laid end to end along the dimension named above; each array names one. Nothing has to cross between parts.
Inputs may be any that keep to these rules, and one draw needn't show every extreme that they name: `gate_lists`: within each panel the 12 entries are distinct; only the first gate_counts entries are used. `gate_counts`: some panel uses all 12 slots. `down_lists`: within each panel the 24 entries are distinct; only the first down_counts entries are used. `down_counts`: some panel uses all 24 slots.
All inputs are finite; a program needn't handle non-finite values.
Results may differ from a plain program's by a relative error of at most 0.005.
Values may be sent and summed in bfloat16 or wider, within the bound.
No kernel may reach another device: no remote copies, remote signals or barrier semaphores. Data moves between devices by JAX's collectives and lax.ppermute only.
A program may use at most 192 MiB of HBM per device.

v0:
```python
import jax
import jax.numpy as jnp
from jax import lax
from jax.sharding import PartitionSpec as P


def slot_mask(slot_counts, slot_total):
    slots = jnp.arange(slot_total, dtype=jnp.int32)
    return (slots < slot_counts[..., None]).astype(jnp.bfloat16)


def local(tokens, gate_tiles, gate_lists, gate_counts, down_tiles, down_lists, down_counts):
    block = gate_tiles.shape[3]
    columns = lax.axis_size("col")
    local_hidden = gate_tiles.shape[0]
    all_tokens = lax.all_gather(tokens, "row", axis=0, tiled=True)
    total_rows = all_tokens.shape[0]
    quarter = total_rows // columns
    lists_here = gate_lists[:, 0, :]
    keep_gate = slot_mask(gate_counts[:, 0], gate_lists.shape[2])
    tiles_here = gate_tiles[:, 0]
    row_count = all_tokens.shape[0]
    blocks_grid = all_tokens.reshape(row_count, -1, block)
    chosen = blocks_grid[:, lists_here, :] * keep_gate[None, :, :, None]
    product = jnp.einsum("rhsk,hskc->rhc", chosen, tiles_here, preferred_element_type=jnp.float32)
    summed = lax.psum(product.reshape(row_count, -1), "col")
    own_rows = lax.dynamic_slice_in_dim(summed, lax.axis_index("col") * quarter, quarter, 0)
    paired = own_rows.reshape(quarter, local_hidden, 2, block)
    hidden = (
        (jax.nn.silu(paired[:, :, 0]) * paired[:, :, 1]).astype(jnp.bfloat16).reshape(quarter, -1)
    )
    hidden_all = lax.all_gather(hidden, "row", axis=1, tiled=True)
    hidden_width = hidden_all.shape[1]
    quarter_blocks = hidden_width // (block * columns)
    tiles_all = lax.all_gather(down_tiles, "col", axis=1, tiled=True)
    lists_all, counts_all = (
        lax.all_gather(down_lists, "col", axis=1, tiled=True),
        lax.all_gather(down_counts, "col", axis=1, tiled=True),
    )
    offsets = (jnp.arange(columns, dtype=jnp.int32) * quarter_blocks)[None, :, None]
    block_index = lists_all + offsets
    keep_down = slot_mask(counts_all, lists_all.shape[2])
    blocks_grid = hidden_all.reshape(quarter, -1, block)
    chosen = blocks_grid[:, block_index, :] * keep_down[None, :, :, :, None]
    product = jnp.einsum("tdqsk,dqskc->tdc", chosen, tiles_all, preferred_element_type=jnp.float32)
    result = product.reshape(quarter, -1)
    return result.astype(jnp.bfloat16)


def solution(mesh):
    return jax.shard_map(
        local,
        mesh=mesh,
        in_specs=(
            P(("groups", "row"), "col"),
            P(("groups", "row"), "col", None, None, None),
            P(("groups", "row"), "col", None),
            P(("groups", "row"), "col"),
            P(("groups", "row"), "col", None, None, None),
            P(("groups", "row"), "col", None),
            P(("groups", "row"), "col"),
        ),
        out_specs=P(("groups", "col"), "row"),
        check_vma=False,
    )
```

profile of v0, /device:TPU:0, one launch (start us, length us, event | category | flops | bytes accessed | tf_op | source)
XLA Modules:
  0.0 431.0 jit_solution(15397803045704059399)
XLA Ops:
  6.5 15.8 %all_gather.15 = bf16[64,2048]{1,0:T(8,128)(2,1)S(1)} all-gather(bf16[16,2048]{1,0:T(8,128)(2,1)} %param.7), channel_id=1, replica_groups=mesh['groups'=2,'row'=4,'col'=4] {'row'}, dimensions={0}, use_global_device_ids=true | all-gather | bytes 327680 | tf_op jit(solution)/shard_map/all_gather | solution.py:16
  22.4 0.7 compare_select_fusion.1
  23.1 0.1 copy.36
  23.2 0.1 reshape.84
  23.3 0.7 fusion.27
  24.1 13.3 %gather_fusion = bf16[384,64,128]{2,1,0:T(8,128)(2,1)} fusion(bf16[64,16,128]{2,0,1:T(8,128)(2,1)S(1)} %copy_bitcast_fusion.1, s32[1024]{0:T(1024)S(1)} %pad_clamp_fusion.1), kind=kCustom, calls=%fused_computation | custom fusion | bytes 12584448 | tf_op jit(solution)/shard_map/gather | solution.py:24
  37.4 12.6 %fusion.8 = f32[32,8,8,256]{3,2,1,0:T(8,128)S(1)} fusion(bf16[32,1,12,128,256]{4,3,2,1,0:T(8,128)(2,1)} %param.8, bf16[32,12,64,128]{3,2,1,0:T(8,128)(2,1)} %bitcast.83, bf16[32,12]{1,0:T(8,128)(2,1)S(1)} %fusion.27), kind=kOutput, calls=%fused_computation.11 | convolution fusion | flops 1613758464 | bytes 33555200 | tf_op jit(solution)/shard_map/rhsk,hskc->rhc/dot_general | solution.py:25
  50.0 1.5 copy.49
  51.7 0.7 all-gather.3.cloned.1.call-update
  52.4 5.2 %all_gather.17 = s32[16,4,24]{2,0,1:T(8,128)S(1)} all-gather(s32[16,1,24]{2,0,1:T(8,128)S(1)} %bitcast.89), channel_id=1, replica_groups=mesh['groups'=2,'row'=4,'col'=4] {'col'}, dimensions={1}, use_global_device_ids=true | all-gather | bytes 7680 | tf_op jit(solution)/shard_map/all_gather | solution.py:37
  57.6 0.1 compare_select_fusion
  57.7 0.1 reshape.92
  57.8 5.0 %all-gather = s32[4,1,16]{2,1,0:T(1,128)S(1)} all-gather(s32[1,1,16]{2,1,0:T(1,128)S(1)} %bitcast.92), channel_id=1, replica_groups=mesh['groups'=2,'row'=4,'col'=4] {'col'}, dimensions={0}, use_global_device_ids=true | all-gather | bytes 320 | tf_op jit(solution)/shard_map/all_gather | solution.py:38
  62.9 41.8 %all-reduce.2.cloned.1.call-done = f32[64,8192]{1,0:T(8,128)} async-done(((f32[64,8192]{1,0:T(8,128)}), f32[64,8192]{1,0:T(8,128)}) %all-reduce.2.cloned.1.call-update) | async-done | bytes 2097168 | tf_op jit(solution)/shard_map/psum | solution.py:26
  104.7 1.1 constant_dynamic-slice_fusion
  105.8 0.4 reshape.80
  106.2 1.3 slice_reduce_fusion.1
  107.6 0.3 fusion.22
  107.9 15.7 %all_gather.16 = bf16[16,16384]{1,0:T(8,128)(2,1)S(1)} all-gather(bf16[16,4096]{1,0:T(8,128)(2,1)S(1)} %fusion.22), channel_id=1, replica_groups=mesh['groups'=2,'row'=4,'col'=4] {'row'}, dimensions={1}, use_global_device_ids=true | all-gather | bytes 655360 | tf_op jit(solution)/shard_map/all_gather | solution.py:32
  123.5 0.1 copy_bitcast_fusion
  123.6 5.7 %gather_fusion.1 = bf16[1536,16,128]{2,1,0:T(8,128)(2,1)} fusion(bf16[16,128,128]{2,0,1:T(8,128)(2,1)S(1)} %copy_bitcast_fusion, s32[2048]{0:T(1024)S(1)} %pad_clamp_fusion), kind=kCustom, calls=%fused_computation.1 | custom fusion | bytes 12589056 | tf_op jit(solution)/shard_map/gather | solution.py:44
  129.3 274.2 %all-gather.3.cloned.1.call-done = bf16[16,4,24,128,128]{4,3,2,0,1:T(8,128)(2,1)} async-done(((bf16[16,1,24,128,128]{4,3,2,0,1:T(8,128)(2,1)}), bf16[16,4,24,128,128]{4,3,2,0,1:T(8,128)(2,1)}) %all-gather.3.cloned.1.call-update) | async-done | bytes 50331664 | tf_op jit(solution)/shard_map/all_gather | solution.py:35
  403.6 19.9 %fusion.19 = bf16[16,2,8,128]{3,2,1,0:T(8,128)(2,1)S(1)} fusion(bf16[16,4,24,128,128]{4,3,2,0,1:T(8,128)(2,1)} %all-gather.3.cloned.1.call-done, bf16[16,4,24,16,128]{4,3,2,1,0:T(8,128)(2,1)} %bitcast.84, bf16[16,4,24]{2,0,1:T(8,128)(2,1)S(1)} %fusion.26), kind=kOutput, calls=%fused_computation.14 | convolution fusion | flops 808484864 | bytes 56691712 | tf_op jit(solution)/shard_map/tdqsk,dqskc->tdc/dot_general | solution.py:45
  423.5 0.6 copy.68
  (13 shorter events, 0.2 us)
Async XLA Ops:
  6.5 98.2 %all-reduce.2.cloned.1.call-start = ((), (), s32[]{:S(2)}) async-start(), calls=%async_computation | async-start | bytes 4194304 | tf_op jit(solution)/shard_map/psum | solution.py:26
  51.6 352.0 %all-gather.3.cloned.1.call-start = ((), (), s32[]{:S(2)}) async-start(), calls=%async_computation.1 | async-start | bytes 62914560 | tf_op jit(solution)/shard_map/all_gather | solution.py:35
  51.6 0.7 copy-start
  51.7 6.1 %copy-start.1 = (s32[16,1]{0,1:T(1,128)S(1)}, s32[16,1]{0,1:T(1,128)}, u32[]{:S(2)}) copy-start(s32[16,1]{0,1:T(1,128)} %param.13) | copy-start | bytes 196
Sparse Core Ops, SparseCore 0:
  51.7 52.9 all-reduce.1
  106.3 297.1 all-gather.2
where the time goes:
time: 431 us
  waiting for transfers between devices  317 us (74%)
  blocking collectives  41.7 us (10%)
  matrix products  32.5 us (8%)
  local copies, waits for them, and re-layouts  24.5 us (6%)
  between operations  13.5 us (3%)
    all_gather x1, waiting for transfers between devices, local(): tiles_all = lax.all_gather(down_tiles, 'col', axis=1, tiled=True)  274 us
    psum x1, waiting for transfers between devices, local(): summed = lax.psum(product.reshape(row_count, -1), 'col')  41.8 us
    dot_general x1, matrix products, local(): jnp.einsum('tdqsk,dqskc->tdc', chosen, tiles_all, preferred_element_type=...  19.9 us
    all_gather x1, blocking collectives, local(): all_tokens = lax.all_gather(tokens, 'row', axis=0, tiled=True)  15.8 us
    all_gather x1, blocking collectives, local(): hidden_all = lax.all_gather(hidden, 'row', axis=1, tiled=True)  15.7 us
    gather x1, local copies, waits for them, and re-layouts, local(): chosen = blocks_grid[:, lists_here, :] * keep_gate[None, :, :, None]  13.3 us
    dot_general x1, matrix products, local(): jnp.einsum('rhsk,hskc->rhc', chosen, tiles_here, preferred_element_type=j...  12.6 us
  transfers between devices with their start and end apart: 2, of which 2 were waited for; matrix products, arithmetic and copies ran while one was open for 2% of the time, Pallas kernels for 0%

commit v1 on v0

v1 whole, which is shorter than its diff:
```python
import functools

import jax
import jax.numpy as jnp
from jax import lax
from jax.experimental import pallas as pl
from jax.experimental.pallas import tpu as pltpu
from jax.sharding import PartitionSpec as P

VMEM = pl.BlockSpec(memory_space=pltpu.VMEM)
SMEM = pl.BlockSpec(memory_space=pltpu.SMEM)
ANY = pl.BlockSpec(memory_space=pl.ANY)


def sparse_kernel(pieces, fan, cap, least, width, x_ref_list, counts, lists, where, tiles, outs, xs, wbuf, acc, sems):
    panels = tiles.shape[0]
    blocks, rows, block = xs.shape
    pairs_least = max(1, least // 2)
    pairs_most = cap // 2

    def pairs_of(panel):
        return jnp.clip((counts[panel, 0] + 1) // 2, pairs_least, pairs_most)

    def copy(panel, pair):
        slots = pl.ds(pair * 2, 2)
        return pltpu.make_async_copy(tiles.at[panel, 0, slots], wbuf.at[panel, slots], sems.at[panel])

    def issue(panel, carry):
        def one(pair, c):
            copy(panel, pair).start()
            return c

        return lax.fori_loop(0, pairs_of(panel), one, carry)

    lax.fori_loop(0, panels, issue, 0)

    for i in range(pieces):
        part_rows = x_ref_list[i].shape[0]
        at = pl.ds(pl.multiple_of(where[i], 16), part_rows)
        for b in range(blocks):
            xs[b, at, :] = x_ref_list[i][:, b * block : (b + 1) * block]

    def work(panel, carry):
        pairs = pairs_of(panel)
        count = counts[panel, 0]

        def one(pair, c):
            copy(panel, pair).wait()
            return c

        lax.fori_loop(0, pairs, one, 0)
        for p in range(pairs_least, pairs_most + 1):

            @pl.when(pairs == p)
            def _(p=p):
                chosen = []
                for s in range(2 * p):
                    x = xs[lists[panel, 0, s]]
                    if s == 2 * p - 1 or s >= least:
                        x = jnp.where(count > s, x, jnp.zeros_like(x))
                    chosen.append(x)
                lhs = jnp.concatenate(chosen, axis=1)
                rhs = wbuf[panel, : 2 * p].reshape(2 * p * block, width)
                acc[...] = jnp.dot(lhs, rhs, preferred_element_type=jnp.float32)

        lanes = pl.ds(pl.multiple_of(panel * width, width), width)
        for k in range(fan):
            part = outs[k].shape[0]
            at = pl.ds(pl.multiple_of(where[pieces + k], 16), part)
            outs[k][:, lanes] = acc[at, :].astype(outs[k].dtype)
        return carry

    lax.fori_loop(0, panels, work, 0)


def sparse_product(xs, offsets, out_offsets, counts, lists, tiles, least):
    panels, _, cap, block, width = tiles.shape
    rows = sum(x.shape[0] for x in xs)
    blocks = xs[0].shape[1] // block
    fan = len(out_offsets)
    pieces = len(xs)
    where = jnp.stack([jnp.asarray(o, jnp.int32) for o in list(offsets) + list(out_offsets)])

    def body(counts_ref, lists_ref, where_ref, *rest):
        x_refs = rest[:pieces]
        tiles_ref = rest[pieces]
        outs = rest[pieces + 1 : pieces + 1 + fan]
        xs_buf, wbuf, acc, sems = rest[pieces + 1 + fan :]
        sparse_kernel(pieces, fan, cap, least, width, x_refs, counts_ref, lists_ref, where_ref, tiles_ref, outs, xs_buf, wbuf, acc, sems)

    return pl.pallas_call(
        body,
        out_shape=[jax.ShapeDtypeStruct((rows // fan, panels * width), jnp.float32 if k == 0 else jnp.bfloat16) for k in range(fan)],
        in_specs=[SMEM, SMEM, SMEM] + [VMEM] * pieces + [ANY],
        out_specs=[VMEM] * fan,
        scratch_shapes=[
            pltpu.VMEM((blocks, rows, block), jnp.bfloat16),
            pltpu.VMEM((panels, cap, block, width), jnp.bfloat16),
            pltpu.VMEM((rows, width), jnp.float32),
            pltpu.SemaphoreType.DMA((panels,)),
        ],
        compiler_params=pltpu.CompilerParams(vmem_limit_bytes=56 * 1024 * 1024),
    )(counts, lists, where, *xs, tiles)


def shifted(x, axis, size, k):
    return lax.ppermute(x, axis, [(i, (i + k) % size) for i in range(size)])


def exchange_sum(parts, axis, size):
    total = parts[0]
    for k in range(1, size):
        total = total + shifted(parts[k], axis, size, k).astype(jnp.float32)
    return total


def local(tokens, gate_tiles, gate_lists, gate_counts, down_tiles, down_lists, down_counts):
    cols, rows = lax.axis_size("col"), lax.axis_size("row")
    row, col = lax.axis_index("row"), lax.axis_index("col")
    hidden_blocks, _, _, block, _ = gate_tiles.shape
    own = tokens.shape[0]
    total = own * rows
    part = total // cols
    part_offsets = [((col + k) % cols) * part for k in range(cols)]

    if rows == cols:
        xs = [tokens] + [shifted(tokens, "row", rows, k) for k in range(1, rows)]
        offsets = [((row + rows - k) % rows) * own for k in range(rows)]
    else:
        xs = [lax.all_gather(tokens, "row", axis=0, tiled=True)]
        offsets = [0]
    sums = sparse_product(xs, offsets, part_offsets, gate_counts, gate_lists, gate_tiles, 4)
    paired = exchange_sum(sums, "col", cols).reshape(part, hidden_blocks, 2, block)
    hidden = (jax.nn.silu(paired[:, :, 0]) * paired[:, :, 1]).astype(jnp.bfloat16).reshape(part, -1)

    if rows == cols:
        hs, h_offsets = [], []
        for k in range(cols):
            pairs = [(r * cols + c, ((c + k) % rows) * cols + r) for r in range(rows) for c in range(cols)]
            hs.append(lax.ppermute(hidden, ("row", "col"), pairs))
            h_offsets.append(((row + rows - k) % rows) * part)
    else:
        every = lax.all_gather(hidden, "row", axis=1, tiled=True).reshape(part, cols, -1)
        every = lax.all_to_all(every, "col", 1, 0, tiled=True)
        hs, h_offsets = [every.reshape(total, -1)], [0]
    outs = sparse_product(hs, h_offsets, part_offsets, down_counts, down_lists, down_tiles, 8)
    return exchange_sum(outs, "col", cols).astype(jnp.bfloat16)


def solution(mesh):
    return jax.shard_map(
        local,
        mesh=mesh,
        in_specs=(
            P(("groups", "row"), "col"),
            P(("groups", "row"), "col", None, None, None),
            P(("groups", "row"), "col", None),
            P(("groups", "row"), "col"),
            P(("groups", "row"), "col", None, None, None),
            P(("groups", "row"), "col", None),
            P(("groups", "row"), "col"),
        ),
        out_specs=P(("groups", "col"), "row"),
        check_vma=False,
    )
```

time: 431 us -> 75.2 us (0.17)
  waiting for transfers between devices: 317 us -> 16.3 us
  blocking collectives: 41.7 us -> 0 us
  matrix products: 32.5 us -> 0 us
  starting transfers between devices: 0.04 us -> 26.9 us
  Pallas kernels: 0 us -> 21.6 us
  local copies, waits for them, and re-layouts: 24.5 us -> 6.76 us
  between operations: 13.5 us -> 0.1 us
    all_gather x1 -> x0, waiting for transfers between devices: 274 us -> none  [local(): tiles_all = lax.all_gather(down_tiles, 'col', axis=1, tiled=True)]
    psum x1 -> x0, waiting for transfers between devices: 41.8 us -> none  [local(): summed = lax.psum(product.reshape(row_count, -1), 'col')]
    all_gather x4 -> x0, blocking collectives: 41.7 us -> none  [the longest x1 15.8 us: local(): all_tokens = lax.all_gather(tokens, 'row', axis=0, tiled=True)]
    dot_general x2 -> x0, matrix products: 32.5 us -> none  [the longest x1 19.9 us: local(): jnp.einsum('tdqsk,dqskc->tdc', chosen, tiles_all, preferred_element_type=...]
    ppermute x0 -> x13, starting transfers between devices: none -> 26.9 us  [the longest x9 18.2 us: shifted(): return lax.ppermute(x, axis, [(i, (i + k) % size) for i in range(size)])]
    pallas_call x0 -> x2, Pallas kernels: none -> 21.6 us  [sparse_product(): pl.pallas_call(body, out_shape=[jax.ShapeDtypeStruct((rows // fan, panels...]
    gather x2 -> x0, local copies, waits for them, and re-layouts: 19 us -> none  [the longest x1 13.3 us: local(): chosen = blocks_grid[:, lists_here, :] * keep_gate[None, :, :, None]]
    ppermute x0 -> x13, waiting for transfers between devices: none -> 16.3 us  [the longest x9 13 us: shifted(): return lax.ppermute(x, axis, [(i, (i + k) % size) for i in range(size)])]
  transfers between devices with their start and end apart: 2 -> 13, of which waited for: 2 -> 8; matrix products, arithmetic and copies ran while one was open for 2% -> 5% of each run, Pallas kernels for 0% -> 0%
where the time goes in v1:
time: 75.2 us; the launch traced here: 74.8 us
  starting transfers between devices  26.9 us (36%)
  Pallas kernels  21.6 us (29%)
  waiting for transfers between devices  16.3 us (22%)
  local copies, waits for them, and re-layouts  6.76 us (9%)
  other arithmetic  3.04 us (4%)
    pallas_call x2, Pallas kernels, sparse_product(): pl.pallas_call(body, out_shape=[jax.ShapeDtypeStruct((rows // fan, panels...  21.6 us
    ppermute x9, starting transfers between devices, shifted(): return lax.ppermute(x, axis, [(i, (i + k) % size) for i in range(size)])  18.2 us
    ppermute x9, waiting for transfers between devices, shifted(): return lax.ppermute(x, axis, [(i, (i + k) % size) for i in range(size)])  13 us
    ppermute x4, starting transfers between devices, local(): hs.append(lax.ppermute(hidden, ('row', 'col'), pairs))  8.69 us
    unnamed x19, local copies, waits for them, and re-layouts  5.09 us
    ppermute x4, waiting for transfers between devices, local(): hs.append(lax.ppermute(hidden, ('row', 'col'), pairs))  3.31 us
    convert_element_type x1, other arithmetic, local(): return exchange_sum(outs, 'col', cols).astype(jnp.bfloat16)  1.57 us
  transfers between devices with their start and end apart: 13, of which 8 were waited for; matrix products, arithmetic and copies ran while one was open for 5% of the time, Pallas kernels for 0%

profile of v1, /device:TPU:0, one launch (start us, length us, event | category | flops | bytes accessed | tf_op | source)
XLA Modules:
  0.0 74.8 jit_solution(11483931154131035765)
XLA Ops:
  0.0 3.0 %collective-permute-start = (bf16[16,2048]{1,0:T(8,128)(2,1)}, bf16[16,2048]{1,0:T(8,128)(2,1)S(1)}, u32[]{:S(2)}, u32[]{:S(2)}) collective-permute-start(bf16[16,2048]{1,0:T(8,128)(2,1)} %rest_0_.1), channel_id=1, source_target_pairs={{0,4},{4,8},{8,12},{12,0},{1,5},{5,9},{9,13},{13,1},{2,6},{6,10},{... | collective-permute-start | bytes 196616 | tf_op jit(solution)/shard_map/ppermute | solution.py:107
  3.0 2.6 %collective-permute-start.1 = (bf16[16,2048]{1,0:T(8,128)(2,1)}, bf16[16,2048]{1,0:T(8,128)(2,1)S(1)}, u32[]{:S(2)}, u32[]{:S(2)}) collective-permute-start(bf16[16,2048]{1,0:T(8,128)(2,1)} %rest_0_.1), channel_id=1, source_target_pairs={{0,8},{4,12},{8,0},{12,4},{1,9},{5,13},{9,1},{13,5},{2,10},{6,14},... | collective-permute-start | bytes 196616 | tf_op jit(solution)/shard_map/ppermute | solution.py:107
  5.6 1.3 %collective-permute-start.2 = (bf16[16,2048]{1,0:T(8,128)(2,1)}, bf16[16,2048]{1,0:T(8,128)(2,1)S(1)}, u32[]{:S(2)}, u32[]{:S(2)}) collective-permute-start(bf16[16,2048]{1,0:T(8,128)(2,1)} %rest_0_.1), channel_id=1, source_target_pairs={{0,12},{4,0},{8,4},{12,8},{1,13},{5,1},{9,5},{13,9},{2,14},{6,2},{... | collective-permute-start | bytes 196616 | tf_op jit(solution)/shard_map/ppermute | solution.py:107
  7.0 1.3 %copy.8.counts_ref = s32[32,1]{1,0:T(8,128)} copy(s32[32,1]{0,1:T(1,128)} %param.10) | data formatting | bytes 256 | tf_op args[3]
  8.3 1.4 %copy.9.lists_ref = s32[32,1,12]{2,1,0:T(1,128)} copy(s32[32,1,12]{0,1,2:T(1,128)} %param.9) | data formatting | bytes 3072 | tf_op args[2]
  11.6 13.4 %shard_map.73 = (f32[16,8192]{1,0:T(8,128)}, bf16[16,8192]{1,0:T(8,128)(2,1)}, bf16[16,8192]{1,0:T(8,128)(2,1)}, bf16[16,8192]{1,0:T(8,128)(2,1)}) custom-call(s32[32,1]{1,0:T(8,128)} %copy.8.counts_ref, s32[32,1,12]{2,1,0:T(1,128)} %copy.9.lists_ref, s32[8]{0:T(128)} %stack.44.where_ref, bf16[16,2048]{1,0:T(8,128)(2,1)} %rest_0_.1, ...), custom_call_target="tpu_custom_call" | custom-call | tf_op jit(solution)/shard_map/pallas_call | solution.py:91
  25.0 1.3 %collective-permute-start.4 = (bf16[16,8192]{1,0:T(8,128)(2,1)}, bf16[16,8192]{1,0:T(8,128)(2,1)S(1)}, u32[]{:S(2)}, u32[]{:S(2)}) collective-permute-start(bf16[16,8192]{1,0:T(8,128)(2,1)} %get-tuple-element.15), channel_id=1, source_target_pairs={{0,2},{1,3},{2,0},{3,1},{4,6},{5,7},{6,4},{7,5},{8,10},{9,11},{10,... | collective-permute-start | bytes 786440 | tf_op jit(solution)/shard_map/ppermute | solution.py:107
  26.3 1.4 %collective-permute-start.5 = (bf16[16,8192]{1,0:T(8,128)(2,1)}, bf16[16,8192]{1,0:T(8,128)(2,1)S(1)}, u32[]{:S(2)}, u32[]{:S(2)}) collective-permute-start(bf16[16,8192]{1,0:T(8,128)(2,1)} %get-tuple-element.16), channel_id=1, source_target_pairs={{0,3},{1,0},{2,1},{3,2},{4,7},{5,4},{6,5},{7,6},{8,11},{9,8},{10,9... | collective-permute-start | bytes 786440 | tf_op jit(solution)/shard_map/ppermute | solution.py:107
  27.7 5.5 %collective-permute-done.3 = bf16[16,8192]{1,0:T(8,128)(2,1)S(1)} collective-permute-done((bf16[16,8192]{1,0:T(8,128)(2,1)}, bf16[16,8192]{1,0:T(8,128)(2,1)S(1)}, u32[]{:S(2)}, u32[]{:S(2)}) %collective-permute-start.3) | collective-permute-done | bytes 262176 | tf_op jit(solution)/shard_map/ppermute | solution.py:107
  33.2 1.2 %collective-permute-done.4 = bf16[16,8192]{1,0:T(8,128)(2,1)S(1)} collective-permute-done((bf16[16,8192]{1,0:T(8,128)(2,1)}, bf16[16,8192]{1,0:T(8,128)(2,1)S(1)}, u32[]{:S(2)}, u32[]{:S(2)}) %collective-permute-start.4) | collective-permute-done | bytes 262176 | tf_op jit(solution)/shard_map/ppermute | solution.py:107
  34.4 3.8 %collective-permute-done.5 = bf16[16,8192]{1,0:T(8,128)(2,1)S(1)} collective-permute-done((bf16[16,8192]{1,0:T(8,128)(2,1)}, bf16[16,8192]{1,0:T(8,128)(2,1)S(1)}, u32[]{:S(2)}, u32[]{:S(2)}) %collective-permute-start.5) | collective-permute-done | bytes 262176 | tf_op jit(solution)/shard_map/ppermute | solution.py:107
  38.3 1.1 %convert_add_fusion = f32[16,8192]{1,0:T(8,128)S(1)} fusion(bf16[16,8192]{1,0:T(8,128)(2,1)S(1)} %collective-permute-done.5, bf16[16,8192]{1,0:T(8,128)(2,1)S(1)} %collective-permute-done.4, f32[16,8192]{1,0:T(8,128)} %get-tuple-element.13, bf16[16,8192]{1,0:T(8,128)(2,1)S(1)} %collective-permute-done.3), kind=kLoop, calls=%fused_computation | loop fusion | flops 786432 | bytes 1835008 | tf_op jit(solution)/shard_map/add | solution.py:113
  41.4 3.9 %collective-permute-start.7 = (bf16[16,4096]{1,0:T(8,128)(2,1)S(1)}, bf16[16,4096]{1,0:T(8,128)(2,1)S(1)}, u32[]{:S(2)}, u32[]{:S(2)}) collective-permute-start(bf16[16,4096]{1,0:T(8,128)(2,1)S(1)} %fusion), channel_id=1, source_target_pairs={{0,4},{1,8},{2,12},{3,0},{4,5},{5,9},{6,13},{7,1},{8,6},{9,10},{10... | collective-permute-start | bytes 393224 | tf_op jit(solution)/shard_map/ppermute | solution.py:140
  45.4 2.1 %collective-permute-start.8 = (bf16[16,4096]{1,0:T(8,128)(2,1)S(1)}, bf16[16,4096]{1,0:T(8,128)(2,1)S(1)}, u32[]{:S(2)}, u32[]{:S(2)}) collective-permute-start(bf16[16,4096]{1,0:T(8,128)(2,1)S(1)} %fusion), channel_id=1, source_target_pairs={{0,8},{1,12},{2,0},{3,4},{4,9},{5,13},{6,1},{7,5},{8,10},{9,14},{1... | collective-permute-start | bytes 393224 | tf_op jit(solution)/shard_map/ppermute | solution.py:140
  47.4 2.0 %collective-permute-start.9 = (bf16[16,4096]{1,0:T(8,128)(2,1)S(1)}, bf16[16,4096]{1,0:T(8,128)(2,1)S(1)}, u32[]{:S(2)}, u32[]{:S(2)}) collective-permute-start(bf16[16,4096]{1,0:T(8,128)(2,1)S(1)} %fusion), channel_id=1, source_target_pairs={{0,12},{1,0},{2,4},{3,8},{4,13},{5,1},{6,5},{7,9},{8,14},{9,2},{10... | collective-permute-start | bytes 393224 | tf_op jit(solution)/shard_map/ppermute | solution.py:140
  50.2 2.2 %collective-permute-done.8.rest_2_ = bf16[16,4096]{1,0:T(8,128)(2,1)S(1)} collective-permute-done((bf16[16,4096]{1,0:T(8,128)(2,1)S(1)}, bf16[16,4096]{1,0:T(8,128)(2,1)S(1)}, u32[]{:S(2)}, u32[]{:S(2)}) %collective-permute-start.8) | collective-permute-done | bytes 131104 | tf_op jit(solution)/shard_map/ppermute | solution.py:140
  52.4 1.1 %collective-permute-done.9.rest_3_ = bf16[16,4096]{1,0:T(8,128)(2,1)S(1)} collective-permute-done((bf16[16,4096]{1,0:T(8,128)(2,1)S(1)}, bf16[16,4096]{1,0:T(8,128)(2,1)S(1)}, u32[]{:S(2)}, u32[]{:S(2)}) %collective-permute-start.9) | collective-permute-done | bytes 131104 | tf_op jit(solution)/shard_map/ppermute | solution.py:140
  54.1 8.3 %shard_map.74 = (f32[16,2048]{1,0:T(8,128)}, bf16[16,2048]{1,0:T(8,128)(2,1)}, bf16[16,2048]{1,0:T(8,128)(2,1)}, bf16[16,2048]{1,0:T(8,128)(2,1)}) custom-call(s32[16,1]{1,0:T(8,128)} %copy.12.counts_ref, s32[16,1,24]{2,1,0:T(1,128)} %lists_ref.2, s32[8]{0:T(128)} %stack.44.where_ref, bf16[16,4096]{1,0:T(8,128)(2,1)} %copy-done, bf16[16,4096]{1,0:T(8,128)(2,1)} %copy-done.1, ...), custom_call_target="tpu_custom_call" | custom-call | tf_op jit(solution)/shard_map/pallas_call | solution.py:91
  62.4 2.6 %collective-permute-start.10 = (bf16[16,2048]{1,0:T(8,128)(2,1)}, bf16[16,2048]{1,0:T(8,128)(2,1)S(1)}, u32[]{:S(2)}, u32[]{:S(2)}) collective-permute-start(bf16[16,2048]{1,0:T(8,128)(2,1)} %get-tuple-element.18), channel_id=1, source_target_pairs={{0,1},{1,2},{2,3},{3,0},{4,5},{5,6},{6,7},{7,4},{8,9},{9,10},{10,1... | collective-permute-start | bytes 196616 | tf_op jit(solution)/shard_map/ppermute | solution.py:107
  65.0 4.6 %collective-permute-start.11 = (bf16[16,2048]{1,0:T(8,128)(2,1)}, bf16[16,2048]{1,0:T(8,128)(2,1)S(1)}, u32[]{:S(2)}, u32[]{:S(2)}) collective-permute-start(bf16[16,2048]{1,0:T(8,128)(2,1)} %get-tuple-element.19), channel_id=1, source_target_pairs={{0,2},{1,3},{2,0},{3,1},{4,6},{5,7},{6,4},{7,5},{8,10},{9,11},{10,... | collective-permute-start | bytes 196616 | tf_op jit(solution)/shard_map/ppermute | solution.py:107
  69.6 1.4 %collective-permute-start.12 = (bf16[16,2048]{1,0:T(8,128)(2,1)}, bf16[16,2048]{1,0:T(8,128)(2,1)S(1)}, u32[]{:S(2)}, u32[]{:S(2)}) collective-permute-start(bf16[16,2048]{1,0:T(8,128)(2,1)} %get-tuple-element.20), channel_id=1, source_target_pairs={{0,3},{1,0},{2,1},{3,2},{4,7},{5,4},{6,5},{7,6},{8,11},{9,8},{10,9... | collective-permute-start | bytes 196616 | tf_op jit(solution)/shard_map/ppermute | solution.py:107
  71.0 1.4 %collective-permute-done.11 = bf16[16,2048]{1,0:T(8,128)(2,1)S(1)} collective-permute-done((bf16[16,2048]{1,0:T(8,128)(2,1)}, bf16[16,2048]{1,0:T(8,128)(2,1)S(1)}, u32[]{:S(2)}, u32[]{:S(2)}) %collective-permute-start.11) | collective-permute-done | bytes 65568 | tf_op jit(solution)/shard_map/ppermute | solution.py:107
  72.3 0.9 %collective-permute-done.12 = bf16[16,2048]{1,0:T(8,128)(2,1)S(1)} collective-permute-done((bf16[16,2048]{1,0:T(8,128)(2,1)}, bf16[16,2048]{1,0:T(8,128)(2,1)S(1)}, u32[]{:S(2)}, u32[]{:S(2)}) %collective-permute-start.12) | collective-permute-done | bytes 65568 | tf_op jit(solution)/shard_map/ppermute | solution.py:107
  73.2 1.6 %add_convert_fusion = bf16[16,2048]{1,0:T(8,128)(2,1)} fusion(bf16[16,2048]{1,0:T(8,128)(2,1)S(1)} %collective-permute-done.12, bf16[16,2048]{1,0:T(8,128)(2,1)S(1)} %collective-permute-done.11, f32[16,2048]{1,0:T(8,128)} %get-tuple-element.17, bf16[16,2048]{1,0:T(8,128)(2,1)S(1)} %collective-permute-done.10), kind=kLoop, calls=%fused_computation.8 | loop fusion | flops 229376 | bytes 393216 | tf_op jit(solution)/shard_map/convert_element_type | solution.py:147
  (29 shorter events, 5.3 us)
Async XLA Ops:
  0.0 49.5 %copy-start.7 = (s32[16,1]{0,1:T(1,128)S(1)}, s32[16,1]{0,1:T(1,128)}, u32[]{:S(2)}) copy-start(s32[16,1]{0,1:T(1,128)} %param.13) | copy-start | bytes 196
  0.0 10.3 %collective-permute-start = (bf16[16,2048]{1,0:T(8,128)(2,1)}, bf16[16,2048]{1,0:T(8,128)(2,1)S(1)}, u32[]{:S(2)}, u32[]{:S(2)}) collective-permute-start(bf16[16,2048]{1,0:T(8,128)(2,1)} %rest_0_.1), channel_id=1, source_target_pairs={{0,4},{4,8},{8,12},{12,0},{1,5},{5,9},{9,13},{13,1},{2,6},{6,10},{... | collective-permute-start | bytes 196616 | tf_op jit(solution)/shard_map/ppermute | solution.py:107
  3.0 7.3 %collective-permute-start.1 = (bf16[16,2048]{1,0:T(8,128)(2,1)}, bf16[16,2048]{1,0:T(8,128)(2,1)S(1)}, u32[]{:S(2)}, u32[]{:S(2)}) collective-permute-start(bf16[16,2048]{1,0:T(8,128)(2,1)} %rest_0_.1), channel_id=1, source_target_pairs={{0,8},{4,12},{8,0},{12,4},{1,9},{5,13},{9,1},{13,5},{2,10},{6,14},... | collective-permute-start | bytes 196616 | tf_op jit(solution)/shard_map/ppermute | solution.py:107
  5.6 4.9 %collective-permute-start.2 = (bf16[16,2048]{1,0:T(8,128)(2,1)}, bf16[16,2048]{1,0:T(8,128)(2,1)S(1)}, u32[]{:S(2)}, u32[]{:S(2)}) collective-permute-start(bf16[16,2048]{1,0:T(8,128)(2,1)} %rest_0_.1), channel_id=1, source_target_pairs={{0,12},{4,0},{8,4},{12,8},{1,13},{5,1},{9,5},{13,9},{2,14},{6,2},{... | collective-permute-start | bytes 196616 | tf_op jit(solution)/shard_map/ppermute | solution.py:107
  10.3 0.6 copy-start.4
  10.4 0.6 copy-start.5
  11.0 0.6 copy-start.6
  25.0 8.3 %collective-permute-start.3 = (bf16[16,8192]{1,0:T(8,128)(2,1)}, bf16[16,8192]{1,0:T(8,128)(2,1)S(1)}, u32[]{:S(2)}, u32[]{:S(2)}) collective-permute-start(bf16[16,8192]{1,0:T(8,128)(2,1)} %get-tuple-element.14), channel_id=1, source_target_pairs={{0,1},{1,2},{2,3},{3,0},{4,5},{5,6},{6,7},{7,4},{8,9},{9,10},{10,1... | collective-permute-start | bytes 786440 | tf_op jit(solution)/shard_map/ppermute | solution.py:107
  25.0 9.4 %collective-permute-start.4 = (bf16[16,8192]{1,0:T(8,128)(2,1)}, bf16[16,8192]{1,0:T(8,128)(2,1)S(1)}, u32[]{:S(2)}, u32[]{:S(2)}) collective-permute-start(bf16[16,8192]{1,0:T(8,128)(2,1)} %get-tuple-element.15), channel_id=1, source_target_pairs={{0,2},{1,3},{2,0},{3,1},{4,6},{5,7},{6,4},{7,5},{8,10},{9,11},{10,... | collective-permute-start | bytes 786440 | tf_op jit(solution)/shard_map/ppermute | solution.py:107
  26.3 12.0 %collective-permute-start.5 = (bf16[16,8192]{1,0:T(8,128)(2,1)}, bf16[16,8192]{1,0:T(8,128)(2,1)S(1)}, u32[]{:S(2)}, u32[]{:S(2)}) collective-permute-start(bf16[16,8192]{1,0:T(8,128)(2,1)} %get-tuple-element.16), channel_id=1, source_target_pairs={{0,3},{1,0},{2,1},{3,2},{4,7},{5,4},{6,5},{7,6},{8,11},{9,8},{10,9... | collective-permute-start | bytes 786440 | tf_op jit(solution)/shard_map/ppermute | solution.py:107
  40.8 9.4 %collective-permute-start.6 = (bf16[16,4096]{1,0:T(8,128)(2,1)S(1)}, bf16[16,4096]{1,0:T(8,128)(2,1)S(1)}, u32[]{:S(2)}, u32[]{:S(2)}) collective-permute-start(bf16[16,4096]{1,0:T(8,128)(2,1)S(1)} %fusion), channel_id=1, source_target_pairs={{0,0},{1,4},{2,8},{3,12},{4,1},{5,5},{6,9},{7,13},{8,2},{9,6},{10,... | collective-permute-start | bytes 393224 | tf_op jit(solution)/shard_map/ppermute | solution.py:140
  41.4 8.7 %collective-permute-start.7 = (bf16[16,4096]{1,0:T(8,128)(2,1)S(1)}, bf16[16,4096]{1,0:T(8,128)(2,1)S(1)}, u32[]{:S(2)}, u32[]{:S(2)}) collective-permute-start(bf16[16,4096]{1,0:T(8,128)(2,1)S(1)} %fusion), channel_id=1, source_target_pairs={{0,4},{1,8},{2,12},{3,0},{4,5},{5,9},{6,13},{7,1},{8,6},{9,10},{10... | collective-permute-start | bytes 393224 | tf_op jit(solution)/shard_map/ppermute | solution.py:140
  45.4 7.0 %collective-permute-start.8 = (bf16[16,4096]{1,0:T(8,128)(2,1)S(1)}, bf16[16,4096]{1,0:T(8,128)(2,1)S(1)}, u32[]{:S(2)}, u32[]{:S(2)}) collective-permute-start(bf16[16,4096]{1,0:T(8,128)(2,1)S(1)} %fusion), channel_id=1, source_target_pairs={{0,8},{1,12},{2,0},{3,4},{4,9},{5,13},{6,1},{7,5},{8,10},{9,14},{1... | collective-permute-start | bytes 393224 | tf_op jit(solution)/shard_map/ppermute | solution.py:140
  47.4 6.0 %collective-permute-start.9 = (bf16[16,4096]{1,0:T(8,128)(2,1)S(1)}, bf16[16,4096]{1,0:T(8,128)(2,1)S(1)}, u32[]{:S(2)}, u32[]{:S(2)}) collective-permute-start(bf16[16,4096]{1,0:T(8,128)(2,1)S(1)} %fusion), channel_id=1, source_target_pairs={{0,12},{1,0},{2,4},{3,8},{4,13},{5,1},{6,5},{7,9},{8,14},{9,2},{10... | collective-permute-start | bytes 393224 | tf_op jit(solution)/shard_map/ppermute | solution.py:140
  50.1 3.3 %copy-start = (bf16[16,4096]{1,0:T(8,128)(2,1)}, bf16[16,4096]{1,0:T(8,128)(2,1)S(1)}, u32[]{:S(2)}) copy-start(bf16[16,4096]{1,0:T(8,128)(2,1)S(1)} %collective-permute-done.6.rest_0_) | copy-start | bytes 393220
  50.1 3.3 %copy-start.1 = (bf16[16,4096]{1,0:T(8,128)(2,1)}, bf16[16,4096]{1,0:T(8,128)(2,1)S(1)}, u32[]{:S(2)}) copy-start(bf16[16,4096]{1,0:T(8,128)(2,1)S(1)} %collective-permute-done.7.rest_1_) | copy-start | bytes 393220
  52.4 1.1 %copy-start.2 = (bf16[16,4096]{1,0:T(8,128)(2,1)}, bf16[16,4096]{1,0:T(8,128)(2,1)S(1)}, u32[]{:S(2)}) copy-start(bf16[16,4096]{1,0:T(8,128)(2,1)S(1)} %collective-permute-done.8.rest_2_) | copy-start | bytes 393220
  53.5 0.7 copy-start.3
  62.4 8.6 %collective-permute-start.10 = (bf16[16,2048]{1,0:T(8,128)(2,1)}, bf16[16,2048]{1,0:T(8,128)(2,1)S(1)}, u32[]{:S(2)}, u32[]{:S(2)}) collective-permute-start(bf16[16,2048]{1,0:T(8,128)(2,1)} %get-tuple-element.18), channel_id=1, source_target_pairs={{0,1},{1,2},{2,3},{3,0},{4,5},{5,6},{6,7},{7,4},{8,9},{9,10},{10,1... | collective-permute-start | bytes 196616 | tf_op jit(solution)/shard_map/ppermute | solution.py:107
  65.0 7.3 %collective-permute-start.11 = (bf16[16,2048]{1,0:T(8,128)(2,1)}, bf16[16,2048]{1,0:T(8,128)(2,1)S(1)}, u32[]{:S(2)}, u32[]{:S(2)}) collective-permute-start(bf16[16,2048]{1,0:T(8,128)(2,1)} %get-tuple-element.19), channel_id=1, source_target_pairs={{0,2},{1,3},{2,0},{3,1},{4,6},{5,7},{6,4},{7,5},{8,10},{9,11},{10,... | collective-permute-start | bytes 196616 | tf_op jit(solution)/shard_map/ppermute | solution.py:107
  69.6 3.6 %collective-permute-start.12 = (bf16[16,2048]{1,0:T(8,128)(2,1)}, bf16[16,2048]{1,0:T(8,128)(2,1)S(1)}, u32[]{:S(2)}, u32[]{:S(2)}) collective-permute-start(bf16[16,2048]{1,0:T(8,128)(2,1)} %get-tuple-element.20), channel_id=1, source_target_pairs={{0,3},{1,0},{2,1},{3,2},{4,7},{5,4},{6,5},{7,6},{8,11},{9,8},{10,9... | collective-permute-start | bytes 196616 | tf_op jit(solution)/shard_map/ppermute | solution.py:107

commit v2 on v0

v2 whole, which is shorter than its diff:
```python
import math

import jax
import jax.numpy as jnp
from jax import lax
from jax.experimental import pallas as pl
from jax.experimental.pallas import tpu as pltpu
from jax.sharding import PartitionSpec as P

VMEM = pl.BlockSpec(memory_space=pltpu.VMEM)
SMEM = pl.BlockSpec(memory_space=pltpu.SMEM)


class Panels:
    def __init__(self, panels, cap, least, step):
        self.panels, self.cap, self.least = panels, cap, least
        self.group = math.gcd(panels, 4)
        low, high = max(1, least // 2), cap // 2
        self.sizes = sorted({*range(low, high, step), high})
        self.low, self.step = low, step
        self.entries = panels + panels // self.group

    def level(self, count):
        pairs = jnp.clip((count + 1) // 2, self.low, self.cap // 2)
        return (pairs - self.low + self.step - 1) // self.step

    def fill(self, counts_ref, table_ref):
        levels = [self.level(counts_ref[h]) for h in range(self.panels)]
        kinds = len(self.sizes)
        tally = [sum((lv == k).astype(jnp.int32) for lv in levels) for k in range(kinds)]
        at = [jnp.int32(0)]
        for k in range(kinds - 1):
            at.append(at[k] + tally[k])
        for h, lv in enumerate(levels):
            spot = at[0]
            for k in range(1, kinds):
                spot = jnp.where(lv == k, at[k], spot)
            table_ref[spot] = jnp.int32(h)
            at = [a + (lv == k).astype(jnp.int32) for k, a in enumerate(at)]
        for g in range(self.panels // self.group):
            table_ref[self.panels + g] = self.level(counts_ref[table_ref[(g + 1) * self.group - 1]])


def opening():
    def body(out_ref):
        out_ref[...] = jnp.zeros_like(out_ref)

    return pl.pallas_call(
        body,
        out_shape=jax.ShapeDtypeStruct((8, 128), jnp.float32),
        out_specs=VMEM,
        cost_estimate=pl.CostEstimate(flops=1 << 35, transcendentals=0, bytes_accessed=4096),
        compiler_params=pltpu.CompilerParams(vmem_limit_bytes=1 << 20),
        name="opening",
    )()


def plan(kinds, counts, after):
    def body(*refs):
        for kind, counts_ref, table_ref in zip(kinds, refs, refs[len(kinds) + 1 :]):
            kind.fill(counts_ref, table_ref)

    return pl.pallas_call(
        body,
        out_shape=[jax.ShapeDtypeStruct((kind.entries,), jnp.int32) for kind in kinds],
        in_specs=[SMEM] * len(kinds) + [VMEM],
        out_specs=[SMEM] * len(kinds),
        cost_estimate=pl.CostEstimate(flops=1 << 34, transcendentals=0, bytes_accessed=4096),
        compiler_params=pltpu.CompilerParams(vmem_limit_bytes=1 << 20),
        name="plan",
    )(*counts, after)


def product(kind, xs, chunk_of, counts, lists, slots_first, table, tiles, name):
    panels, cap, block, width = tiles.shape
    rows = sum(x.shape[0] for x in xs)
    blocks = xs[0].shape[1] // block
    pieces = len(xs)
    part = rows // 4
    group = kind.group

    def body(counts_ref, lists_ref, table_ref, *rest):
        x_refs = rest[:pieces]
        tiles_ref, kept, sent, x_all = rest[pieces:]
        col = lax.axis_index("col")
        for t in range(4):
            flip = chunk_of(t) ^ col
            spot = (flip & 1) * 2 + flip // 2
            at = pl.ds(pl.multiple_of(spot * part, 16), part)
            for b in range(blocks):
                lanes = slice(b * block, (b + 1) * block)
                x_all[b, at, :] = x_refs[t][:, lanes] if pieces == 4 else x_refs[0][t * part : (t + 1) * part, lanes]

        @pl.loop(0, panels // group)
        def _(g):
            level = table_ref[panels + g]
            members = [table_ref[g * group + u] for u in range(group)]
            for k, pairs in enumerate(kind.sizes):

                @pl.when(level == k)
                def _(pairs=pairs):
                    for panel in members:
                        count = counts_ref[panel]
                        chosen = []
                        for s in range(2 * pairs):
                            x = x_all[lists_ref[s, 0, panel] if slots_first else lists_ref[panel, 0, s]]
                            if s >= kind.least:
                                x = jnp.where(count > s, x, jnp.zeros_like(x))
                            chosen.append(x)
                        lhs = jnp.concatenate(chosen, axis=1)
                        rhs = tiles_ref[panel, : 2 * pairs].reshape(2 * pairs * block, width)
                        sums = jnp.dot(lhs, rhs, preferred_element_type=jnp.float32)
                        lanes = pl.ds(pl.multiple_of(panel * width, width), width)
                        kept[:, lanes] = sums[: rows // 2]
                        sent[:, lanes] = sums[rows // 2 :].astype(sent.dtype)

    return pl.pallas_call(
        body,
        out_shape=[
            jax.ShapeDtypeStruct((rows // 2, panels * width), jnp.float32),
            jax.ShapeDtypeStruct((rows // 2, panels * width), jnp.bfloat16),
        ],
        in_specs=[SMEM] * 3 + [VMEM] * (pieces + 1),
        out_specs=[VMEM, VMEM],
        scratch_shapes=[pltpu.VMEM((blocks, rows, block), jnp.bfloat16)],
        compiler_params=pltpu.CompilerParams(vmem_limit_bytes=(4 << 20) + rows * blocks * block * 4 + rows * width * 8),
        cost_estimate=pl.CostEstimate(flops=2 * rows * tiles.size, transcendentals=0, bytes_accessed=tiles.size * 2),
        name=name,
    )(counts, lists, table, *xs, tiles)


def elementwise(body, shapes, name, *args):
    return pl.pallas_call(
        body,
        out_shape=shapes,
        in_specs=[VMEM] * len(args),
        out_specs=[VMEM] * len(shapes),
        compiler_params=pltpu.CompilerParams(vmem_limit_bytes=4 << 20),
        name=name,
    )(*args)


def add_halves(kept, got):
    half, width = kept.shape[0] // 2, kept.shape[1]

    def body(kept_ref, got_ref, own_ref, send_ref):
        own_ref[...] = kept_ref[:half] + got_ref[:half].astype(jnp.float32)
        send_ref[...] = (kept_ref[half:] + got_ref[half:].astype(jnp.float32)).astype(jnp.bfloat16)

    shapes = [jax.ShapeDtypeStruct((half, width), jnp.float32), jax.ShapeDtypeStruct((half, width), jnp.bfloat16)]
    return elementwise(body, shapes, "add_halves", kept, got)


def swiglu(own, got, block):
    part, width = own.shape
    panels = width // (2 * block)

    def body(own_ref, got_ref, out_ref):
        for h in range(panels):
            lo = h * 2 * block
            gate = own_ref[:, lo : lo + block] + got_ref[:, lo : lo + block].astype(jnp.float32)
            up = own_ref[:, lo + block : lo + 2 * block] + got_ref[:, lo + block : lo + 2 * block].astype(jnp.float32)
            out_ref[:, h * block : (h + 1) * block] = (gate / (1.0 + jnp.exp(-gate)) * up).astype(jnp.bfloat16)

    return elementwise(body, [jax.ShapeDtypeStruct((part, width // 2), jnp.bfloat16)], "swiglu", own, got)[0]


def last_sum(own, got):
    def body(own_ref, got_ref, out_ref):
        out_ref[...] = (own_ref[...] + got_ref[...].astype(jnp.float32)).astype(jnp.bfloat16)

    return elementwise(body, [jax.ShapeDtypeStruct(own.shape, jnp.bfloat16)], "last_sum", own, got)[0]


def flipped(x, bit):
    return lax.ppermute(x, "col", [(i, i ^ bit) for i in range(4)])


def local(tokens, gate_tiles, gate_lists, gate_counts, down_tiles, down_lists, down_counts):
    cols, rows = lax.axis_size("col"), lax.axis_size("row")
    assert cols == 4
    block = gate_tiles.shape[3]
    total = tokens.shape[0] * rows
    part = total // cols
    square = rows == cols

    gate_kind = Panels(gate_tiles.shape[0], gate_tiles.shape[2], 4, 1)
    down_kind = Panels(down_tiles.shape[0], down_tiles.shape[2], 8, 2)
    gate_used, down_used = gate_counts.reshape(-1), down_counts.reshape(-1)

    def chunk_of(k):
        return lax.rem(lax.axis_index("row") + (rows - k), rows) if square else k

    tokens, opened = lax.optimization_barrier((tokens, opening()))
    if square:
        xs = [tokens] + [lax.ppermute(tokens, "row", [(i, (i + k) % rows) for i in range(rows)]) for k in range(1, rows)]
    else:
        xs = [lax.all_gather(tokens, "row", axis=0, tiled=True)]
    gate_table, down_table = plan([gate_kind, down_kind], [gate_used, down_used], opened)

    kept, sent = product(
        gate_kind, xs, chunk_of, gate_used, jnp.transpose(gate_lists, (2, 1, 0)), True, gate_table, gate_tiles[:, 0], "gate_up"
    )
    summed, crossing = add_halves(kept, flipped(sent, 1))
    hidden = swiglu(summed, flipped(crossing, 2), block)

    if square:
        hs = [
            lax.ppermute(
                hidden, ("row", "col"), [(r * cols + c, ((c + k) % rows) * cols + r) for r in range(rows) for c in range(cols)]
            )
            for k in range(cols)
        ]
    else:
        every = lax.all_gather(hidden, "row", axis=1, tiled=True).reshape(part, cols, -1)
        every = lax.all_to_all(every, "col", 1, 0, tiled=True)
        hs = [every.reshape(total, -1)]
    kept, sent = product(down_kind, hs, chunk_of, down_used, down_lists, False, down_table, down_tiles[:, 0], "down")
    summed, crossing = add_halves(kept, flipped(sent, 1))
    return last_sum(summed, flipped(crossing, 2))


def solution(mesh):
    return jax.shard_map(
        local,
        mesh=mesh,
        in_specs=(
            P(("groups", "row"), "col"),
            P(("groups", "row"), "col", None, None, None),
            P(("groups", "row"), "col", None),
            P(("groups", "row"), "col"),
            P(("groups", "row"), "col", None, None, None),
            P(("groups", "row"), "col", None),
            P(("groups", "row"), "col"),
        ),
        out_specs=P(("groups", "col"), "row"),
        check_vma=False,
    )
```

time: 431 us -> 53.4 us (0.12)
  waiting for transfers between devices: 317 us -> 22.4 us
  blocking collectives: 41.7 us -> 0 us
  matrix products: 32.5 us -> 0 us
  local copies, waits for them, and re-layouts: 24.5 us -> 0.86 us
  starting transfers between devices: 0.04 us -> 18.3 us
  between operations: 13.5 us -> 0.22 us
  Pallas kernels: 0 us -> 11.6 us
    all_gather x1 -> x0, waiting for transfers between devices: 274 us -> none  [local(): tiles_all = lax.all_gather(down_tiles, 'col', axis=1, tiled=True)]
    psum x1 -> x0, waiting for transfers between devices: 41.8 us -> none  [local(): summed = lax.psum(product.reshape(row_count, -1), 'col')]
    all_gather x4 -> x0, blocking collectives: 41.7 us -> none  [the longest x1 15.8 us: local(): all_tokens = lax.all_gather(tokens, 'row', axis=0, tiled=True)]
    dot_general x2 -> x0, matrix products: 32.5 us -> none  [the longest x1 19.9 us: local(): jnp.einsum('tdqsk,dqskc->tdc', chosen, tiles_all, preferred_element_type=...]
    ppermute x0 -> x11, waiting for transfers between devices: none -> 22.4 us  [the longest x4 12.7 us: flipped(): return lax.ppermute(x, 'col', [(i, i ^ bit) for i in range(4)])]
    gather x2 -> x0, local copies, waits for them, and re-layouts: 19 us -> none  [the longest x1 13.3 us: local(): chosen = blocks_grid[:, lists_here, :] * keep_gate[None, :, :, None]]
    ppermute x0 -> x11, starting transfers between devices: none -> 18.3 us  [the longest x4 7.55 us: flipped(): return lax.ppermute(x, 'col', [(i, i ^ bit) for i in range(4)])]
    pallas_call x0 -> x8, Pallas kernels: none -> 11.6 us  [the longest x2 8.62 us: product(): pl.pallas_call(body, out_shape=[jax.ShapeDtypeStruct((rows // 2, panels *...]
  transfers between devices with their start and end apart: 2 -> 11, of which waited for: 2 -> 8; matrix products, arithmetic and copies ran while one was open for 2% -> 0% of each run, Pallas kernels for 0% -> 4%
where the time goes in v2:
time: 53.4 us; the launch traced here: 53.3 us
  waiting for transfers between devices  22.4 us (42%)
  starting transfers between devices  18.3 us (34%)
  Pallas kernels  11.6 us (22%)
  local copies, waits for them, and re-layouts  0.86 us (2%)
    ppermute x4, waiting for transfers between devices, flipped(): return lax.ppermute(x, 'col', [(i, i ^ bit) for i in range(4)])  12.7 us
    pallas_call x2, Pallas kernels, product(): pl.pallas_call(body, out_shape=[jax.ShapeDtypeStruct((rows // 2, panels *...  8.62 us
    ppermute x4, starting transfers between devices, flipped(): return lax.ppermute(x, 'col', [(i, i ^ bit) for i in range(4)])  7.55 us
    ppermute x4, waiting for transfers between devices, local(): lax.ppermute(hidden, ('row', 'col'), [(r * cols + c, (c + k) % rows * col...  6.41 us
    ppermute x3, starting transfers between devices, local(): lax.ppermute(tokens, 'row', [(i, (i + k) % rows) for i in range(rows)])  6.06 us
    ppermute x4, starting transfers between devices, local(): lax.ppermute(hidden, ('row', 'col'), [(r * cols + c, (c + k) % rows * col...  4.67 us
    ppermute x3, waiting for transfers between devices, local(): lax.ppermute(tokens, 'row', [(i, (i + k) % rows) for i in range(rows)])  3.27 us
    pallas_call x1, Pallas kernels, plan(): pl.pallas_call(body, out_shape=[jax.ShapeDtypeStruct((kind.entries,), jnp...  2.12 us
  transfers between devices with their start and end apart: 11, of which 8 were waited for; matrix products, arithmetic and copies ran while one was open for 0% of the time, Pallas kernels for 4%

profile of v2, /device:TPU:0, one launch (start us, length us, event | category | flops | bytes accessed | tf_op | source)
XLA Modules:
  0.0 53.3 jit_solution(5703338171088653115)
XLA Ops:
  0.0 0.8 %copy-done = bf16[16,2048]{1,0:T(8,128)(2,1)S(1)} copy-done((bf16[16,2048]{1,0:T(8,128)(2,1)S(1)}, bf16[16,2048]{1,0:T(8,128)(2,1)}, u32[]{:S(2)}) %copy-start) | copy-done | bytes 65560
  0.8 5.0 %collective-permute-start.2 = (bf16[16,2048]{1,0:T(8,128)(2,1)S(1)}, bf16[16,2048]{1,0:T(8,128)(2,1)S(1)}, u32[]{:S(2)}, u32[]{:S(2)}) collective-permute-start(bf16[16,2048]{1,0:T(8,128)(2,1)S(1)} %copy-done), channel_id=1, source_target_pairs={{0,12},{4,0},{8,4},{12,8},{1,13},{5,1},{9,5},{13,9},{2,14},{6,2},{... | collective-permute-start | bytes 196616 | tf_op jit(solution)/shard_map/ppermute | solution.py:196
  5.9 1.0 %collective-permute-start = (bf16[16,2048]{1,0:T(8,128)(2,1)S(1)}, bf16[16,2048]{1,0:T(8,128)(2,1)S(1)}, u32[]{:S(2)}, u32[]{:S(2)}) collective-permute-start(bf16[16,2048]{1,0:T(8,128)(2,1)S(1)} %copy-done), channel_id=1, source_target_pairs={{0,4},{4,8},{8,12},{12,0},{1,5},{5,9},{9,13},{13,1},{2,6},{6,10},{... | collective-permute-start | bytes 196616 | tf_op jit(solution)/shard_map/ppermute | solution.py:196
  6.9 2.1 %plan.1 = (s32[40]{0:T(128)S(1)}, s32[20]{0:T(128)S(1)}) custom-call(s32[32]{0:T(128)S(1)} %bitcast.12, s32[16]{0:T(128)S(1)} %bitcast.14, f32[8,128]{1,0:T(8,128)S(1)} %opening.1.refs_2_), custom_call_target="tpu_custom_call" | custom-call | flops 17179869184 | bytes 4096 | tf_op jit(solution)/shard_map/plan/pallas_call | solution.py:63
  9.1 3.3 %collective-permute-done.1.rest_2_ = bf16[16,2048]{1,0:T(8,128)(2,1)S(1)} collective-permute-done((bf16[16,2048]{1,0:T(8,128)(2,1)S(1)}, bf16[16,2048]{1,0:T(8,128)(2,1)S(1)}, u32[]{:S(2)}, u32[]{:S(2)}) %collective-permute-start.1) | collective-permute-done | bytes 65568 | tf_op jit(solution)/shard_map/ppermute | solution.py:196
  12.4 5.1 %gate_up.1 = (f32[32,8192]{1,0:T(8,128)S(1)}, bf16[32,8192]{1,0:T(8,128)(2,1)S(1)}) custom-call(s32[32]{0:T(128)S(1)} %bitcast.13, s32[12,1,32]{2,1,0:T(1,128)S(1)} %bitcast.11, s32[40]{0:T(128)S(1)} %get-tuple-element.19.table_ref, bf16[16,2048]{1,0:T(8,128)(2,1)S(1)} %copy-done, bf16[16,2048]{1,0:T(8,128)(2,1)S(1)} %collective-permute-done.rest_1_, ...), custom_call_target="tpu_custom_call" | custom-call | flops 1610612736 | bytes 25165824 | tf_op jit(solution)/shard_map/gate_up/pallas_call | solution.py:117
  17.6 0.1 collective-permute-start.3
  17.7 1.9 %collective-permute-done.3.got_ref = bf16[32,8192]{1,0:T(8,128)(2,1)S(1)} collective-permute-done((bf16[32,8192]{1,0:T(8,128)(2,1)S(1)}, bf16[32,8192]{1,0:T(8,128)(2,1)S(1)}, u32[]{:S(2)}, u32[]{:S(2)}) %collective-permute-start.3) | collective-permute-done | bytes 524320 | tf_op jit(solution)/shard_map/ppermute | solution.py:176
  19.6 0.1 add_halves.2
  19.7 1.4 %collective-permute-start.4 = (bf16[16,8192]{1,0:T(8,128)(2,1)S(1)}, bf16[16,8192]{1,0:T(8,128)(2,1)S(1)}, u32[]{:S(2)}, u32[]{:S(2)}) collective-permute-start(bf16[16,8192]{1,0:T(8,128)(2,1)S(1)} %get-tuple-element.24), channel_id=1, source_target_pairs={{0,2},{1,3},{2,0},{3,1},{4,6},{5,7},{6,4},{7,5},{8,10},{9,11},{10,... | collective-permute-start | bytes 786440 | tf_op jit(solution)/shard_map/ppermute | solution.py:176
  21.0 7.0 %collective-permute-done.4.got_ref = bf16[16,8192]{1,0:T(8,128)(2,1)S(1)} collective-permute-done((bf16[16,8192]{1,0:T(8,128)(2,1)S(1)}, bf16[16,8192]{1,0:T(8,128)(2,1)S(1)}, u32[]{:S(2)}, u32[]{:S(2)}) %collective-permute-start.4) | collective-permute-done | bytes 262176 | tf_op jit(solution)/shard_map/ppermute | solution.py:176
  28.1 0.1 swiglu.1
  28.2 2.0 %collective-permute-start.8 = (bf16[16,4096]{1,0:T(8,128)(2,1)S(1)}, bf16[16,4096]{1,0:T(8,128)(2,1)S(1)}, u32[]{:S(2)}, u32[]{:S(2)}) collective-permute-start(bf16[16,4096]{1,0:T(8,128)(2,1)S(1)} %swiglu.1), channel_id=1, source_target_pairs={{0,12},{1,0},{2,4},{3,8},{4,13},{5,1},{6,5},{7,9},{8,14},{9,2},{10... | collective-permute-start | bytes 393224 | tf_op jit(solution)/shard_map/ppermute | solution.py:209
  30.2 1.1 %collective-permute-start.7 = (bf16[16,4096]{1,0:T(8,128)(2,1)S(1)}, bf16[16,4096]{1,0:T(8,128)(2,1)S(1)}, u32[]{:S(2)}, u32[]{:S(2)}) collective-permute-start(bf16[16,4096]{1,0:T(8,128)(2,1)S(1)} %swiglu.1), channel_id=1, source_target_pairs={{0,8},{1,12},{2,0},{3,4},{4,9},{5,13},{6,1},{7,5},{8,10},{9,14},{1... | collective-permute-start | bytes 393224 | tf_op jit(solution)/shard_map/ppermute | solution.py:209
  31.4 0.8 %collective-permute-start.6 = (bf16[16,4096]{1,0:T(8,128)(2,1)S(1)}, bf16[16,4096]{1,0:T(8,128)(2,1)S(1)}, u32[]{:S(2)}, u32[]{:S(2)}) collective-permute-start(bf16[16,4096]{1,0:T(8,128)(2,1)S(1)} %swiglu.1), channel_id=1, source_target_pairs={{0,4},{1,8},{2,12},{3,0},{4,5},{5,9},{6,13},{7,1},{8,6},{9,10},{10... | collective-permute-start | bytes 393224 | tf_op jit(solution)/shard_map/ppermute | solution.py:209
  32.2 0.7 %collective-permute-start.5 = (bf16[16,4096]{1,0:T(8,128)(2,1)S(1)}, bf16[16,4096]{1,0:T(8,128)(2,1)S(1)}, u32[]{:S(2)}, u32[]{:S(2)}) collective-permute-start(bf16[16,4096]{1,0:T(8,128)(2,1)S(1)} %swiglu.1), channel_id=1, source_target_pairs={{0,0},{1,4},{2,8},{3,12},{4,1},{5,5},{6,9},{7,13},{8,2},{9,6},{10,... | collective-permute-start | bytes 393224 | tf_op jit(solution)/shard_map/ppermute | solution.py:209
  32.9 1.2 %collective-permute-done.8.rest_3_ = bf16[16,4096]{1,0:T(8,128)(2,1)S(1)} collective-permute-done((bf16[16,4096]{1,0:T(8,128)(2,1)S(1)}, bf16[16,4096]{1,0:T(8,128)(2,1)S(1)}, u32[]{:S(2)}, u32[]{:S(2)}) %collective-permute-start.8) | collective-permute-done | bytes 131104 | tf_op jit(solution)/shard_map/ppermute | solution.py:209
  34.1 4.3 %collective-permute-done.7.rest_2_ = bf16[16,4096]{1,0:T(8,128)(2,1)S(1)} collective-permute-done((bf16[16,4096]{1,0:T(8,128)(2,1)S(1)}, bf16[16,4096]{1,0:T(8,128)(2,1)S(1)}, u32[]{:S(2)}, u32[]{:S(2)}) %collective-permute-start.7) | collective-permute-done | bytes 131104 | tf_op jit(solution)/shard_map/ppermute | solution.py:209
  38.4 0.9 %collective-permute-done.6.rest_1_ = bf16[16,4096]{1,0:T(8,128)(2,1)S(1)} collective-permute-done((bf16[16,4096]{1,0:T(8,128)(2,1)S(1)}, bf16[16,4096]{1,0:T(8,128)(2,1)S(1)}, u32[]{:S(2)}, u32[]{:S(2)}) %collective-permute-start.6) | collective-permute-done | bytes 131104 | tf_op jit(solution)/shard_map/ppermute | solution.py:209
  39.3 3.5 %down.1 = (f32[32,2048]{1,0:T(8,128)S(1)}, bf16[32,2048]{1,0:T(8,128)(2,1)S(1)}) custom-call(s32[16]{0:T(128)S(1)} %bitcast.15, s32[16,1,24]{2,1,0:T(1,128)S(1)} %copy-done.1, s32[20]{0:T(128)S(1)} %get-tuple-element.18.table_ref, bf16[16,4096]{1,0:T(8,128)(2,1)S(1)} %collective-permute-done.5.rest_0_, bf16[16,4096]{1,0:T(8,128)(2,1)S(1)} %collective-permute-done.6.rest_1_, ...), custom_call_target="tpu_custom_call" | custom-call | flops 805306368 | bytes 12582912 | tf_op jit(solution)/shard_map/down/pallas_call | solution.py:117
  42.9 1.3 %collective-permute-done.9.got_ref = bf16[32,2048]{1,0:T(8,128)(2,1)S(1)} collective-permute-done((bf16[32,2048]{1,0:T(8,128)(2,1)S(1)}, bf16[32,2048]{1,0:T(8,128)(2,1)S(1)}, u32[]{:S(2)}, u32[]{:S(2)}) %collective-permute-start.9) | collective-permute-done | bytes 131104 | tf_op jit(solution)/shard_map/ppermute | solution.py:176
  44.3 6.0 %collective-permute-start.10 = (bf16[16,2048]{1,0:T(8,128)(2,1)S(1)}, bf16[16,2048]{1,0:T(8,128)(2,1)S(1)}, u32[]{:S(2)}, u32[]{:S(2)}) collective-permute-start(bf16[16,2048]{1,0:T(8,128)(2,1)S(1)} %get-tuple-element.28), channel_id=1, source_target_pairs={{0,2},{1,3},{2,0},{3,1},{4,6},{5,7},{6,4},{7,5},{8,10},{9,11},{10,... | collective-permute-start | bytes 196616 | tf_op jit(solution)/shard_map/ppermute | solution.py:176
  50.3 2.4 %collective-permute-done.10.got_ref = bf16[16,2048]{1,0:T(8,128)(2,1)S(1)} collective-permute-done((bf16[16,2048]{1,0:T(8,128)(2,1)S(1)}, bf16[16,2048]{1,0:T(8,128)(2,1)S(1)}, u32[]{:S(2)}, u32[]{:S(2)}) %collective-permute-start.10) | collective-permute-done | bytes 65568 | tf_op jit(solution)/shard_map/ppermute | solution.py:176
  52.7 0.6 %last_sum.1 = bf16[16,2048]{1,0:T(8,128)(2,1)} custom-call(f32[16,2048]{1,0:T(8,128)S(1)} %get-tuple-element.27.own_ref, bf16[16,2048]{1,0:T(8,128)(2,1)S(1)} %collective-permute-done.10.got_ref), custom_call_target="tpu_custom_call" | custom-call | tf_op jit(solution)/shard_map/last_sum/pallas_call | solution.py:133
  (36 shorter events, 0.2 us)
Async XLA Ops:
  0.0 6.9 %copy-start.4 = (s32[16,1]{0,1:T(1,128)S(1)}, s32[16,1]{0,1:T(1,128)}, u32[]{:S(2)}) copy-start(s32[16,1]{0,1:T(1,128)} %param.13) | copy-start | bytes 196
  0.0 6.9 %copy-start.3 = (s32[32,1]{0,1:T(1,128)S(1)}, s32[32,1]{0,1:T(1,128)}, u32[]{:S(2)}) copy-start(s32[32,1]{0,1:T(1,128)} %param.10) | copy-start | bytes 388
  0.0 12.4 %slice-start = ((s8[25165824]{0:T(1024)(128)(4,1)}), s8[4194304]{0:T(1024)(128)(4,1)S(1)}, s32[]{:S(2)}) async-start(s8[25165824]{0:T(1024)(128)(4,1)} %bitcast.5), calls=%async_computation | async-start | bytes 8388608
  0.0 12.4 %slice-start.1 = ((s8[25165824]{0:T(1024)(128)(4,1)}), s8[4194304]{0:T(1024)(128)(4,1)S(1)}, s32[]{:S(2)}) async-start(s8[25165824]{0:T(1024)(128)(4,1)} %bitcast.5), calls=%async_computation.1 | async-start | bytes 8388608
  0.0 12.4 %slice-start.2 = ((s8[25165824]{0:T(1024)(128)(4,1)}), s8[4194304]{0:T(1024)(128)(4,1)S(1)}, s32[]{:S(2)}) async-start(s8[25165824]{0:T(1024)(128)(4,1)} %bitcast.5), calls=%async_computation.2 | async-start | bytes 8388608
  0.0 12.4 %slice-start.3 = ((s8[25165824]{0:T(1024)(128)(4,1)}), s8[4194304]{0:T(1024)(128)(4,1)S(1)}, s32[]{:S(2)}) async-start(s8[25165824]{0:T(1024)(128)(4,1)} %bitcast.5), calls=%async_computation.3 | async-start | bytes 8388608
  0.8 8.2 %collective-permute-start.2 = (bf16[16,2048]{1,0:T(8,128)(2,1)S(1)}, bf16[16,2048]{1,0:T(8,128)(2,1)S(1)}, u32[]{:S(2)}, u32[]{:S(2)}) collective-permute-start(bf16[16,2048]{1,0:T(8,128)(2,1)S(1)} %copy-done), channel_id=1, source_target_pairs={{0,12},{4,0},{8,4},{12,8},{1,13},{5,1},{9,5},{13,9},{2,14},{6,2},{... | collective-permute-start | bytes 196616 | tf_op jit(solution)/shard_map/ppermute | solution.py:196
  5.9 6.5 %collective-permute-start.1 = (bf16[16,2048]{1,0:T(8,128)(2,1)S(1)}, bf16[16,2048]{1,0:T(8,128)(2,1)S(1)}, u32[]{:S(2)}, u32[]{:S(2)}) collective-permute-start(bf16[16,2048]{1,0:T(8,128)(2,1)S(1)} %copy-done), channel_id=1, source_target_pairs={{0,8},{4,12},{8,0},{12,4},{1,9},{5,13},{9,1},{13,5},{2,10},{6,14},... | collective-permute-start | bytes 196616 | tf_op jit(solution)/shard_map/ppermute | solution.py:196
  5.9 6.5 %collective-permute-start = (bf16[16,2048]{1,0:T(8,128)(2,1)S(1)}, bf16[16,2048]{1,0:T(8,128)(2,1)S(1)}, u32[]{:S(2)}, u32[]{:S(2)}) collective-permute-start(bf16[16,2048]{1,0:T(8,128)(2,1)S(1)} %copy-done), channel_id=1, source_target_pairs={{0,4},{4,8},{8,12},{12,0},{1,5},{5,9},{9,13},{13,1},{2,6},{6,10},{... | collective-permute-start | bytes 196616 | tf_op jit(solution)/shard_map/ppermute | solution.py:196
  6.9 5.5 %slice-start.4 = ((s8[25165824]{0:T(1024)(128)(4,1)}), s8[4194304]{0:T(1024)(128)(4,1)S(1)}, s32[]{:S(2)}) async-start(s8[25165824]{0:T(1024)(128)(4,1)} %bitcast.5), calls=%async_computation.4 | async-start | bytes 8388608
  6.9 5.5 %slice-start.5 = ((s8[25165824]{0:T(1024)(128)(4,1)}), s8[4194304]{0:T(1024)(128)(4,1)S(1)}, s32[]{:S(2)}) async-start(s8[25165824]{0:T(1024)(128)(4,1)} %bitcast.5), calls=%async_computation.5 | async-start | bytes 8388608
  6.9 5.5 %copy-start.2 = (s32[32,1,12]{0,1,2:T(1,128)S(1)}, s32[32,1,12]{0,1,2:T(1,128)}, u32[]{:S(2)}) copy-start(s32[32,1,12]{0,1,2:T(1,128)} %param.9) | copy-start | bytes 4612
  9.1 30.2 %slice-start.6 = ((s8[12582912]{0:T(1024)(128)(4,1)}), s8[4194304]{0:T(1024)(128)(4,1)S(1)}, s32[]{:S(2)}) async-start(s8[12582912]{0:T(1024)(128)(4,1)} %bitcast.8), calls=%async_computation.6 | async-start | bytes 8388608
  9.1 30.2 %copy-start.1 = (s32[16,1,24]{2,1,0:T(1,128)S(1)}, s32[16,1,24]{2,1,0:T(1,128)}, u32[]{:S(2)}) copy-start(s32[16,1,24]{2,1,0:T(1,128)} %lists_ref.1) | copy-start | bytes 4612
  12.4 26.9 %slice-start.7 = ((s8[12582912]{0:T(1024)(128)(4,1)}), s8[4194304]{0:T(1024)(128)(4,1)S(1)}, s32[]{:S(2)}) async-start(s8[12582912]{0:T(1024)(128)(4,1)} %bitcast.8), calls=%async_computation.7 | async-start | bytes 8388608
  12.4 26.9 %slice-start.8 = ((s8[12582912]{0:T(1024)(128)(4,1)}), s8[4194304]{0:T(1024)(128)(4,1)S(1)}, s32[]{:S(2)}) async-start(s8[12582912]{0:T(1024)(128)(4,1)} %bitcast.8), calls=%async_computation.8 | async-start | bytes 8388608
  17.6 2.0 %collective-permute-start.3 = (bf16[32,8192]{1,0:T(8,128)(2,1)S(1)}, bf16[32,8192]{1,0:T(8,128)(2,1)S(1)}, u32[]{:S(2)}, u32[]{:S(2)}) collective-permute-start(bf16[32,8192]{1,0:T(8,128)(2,1)S(1)} %get-tuple-element.22), channel_id=1, source_target_pairs={{0,1},{1,0},{2,3},{3,2},{4,5},{5,4},{6,7},{7,6},{8,9},{9,8},{10,11... | collective-permute-start | bytes 1572872 | tf_op jit(solution)/shard_map/ppermute | solution.py:176
  19.7 8.4 %collective-permute-start.4 = (bf16[16,8192]{1,0:T(8,128)(2,1)S(1)}, bf16[16,8192]{1,0:T(8,128)(2,1)S(1)}, u32[]{:S(2)}, u32[]{:S(2)}) collective-permute-start(bf16[16,8192]{1,0:T(8,128)(2,1)S(1)} %get-tuple-element.24), channel_id=1, source_target_pairs={{0,2},{1,3},{2,0},{3,1},{4,6},{5,7},{6,4},{7,5},{8,10},{9,11},{10,... | collective-permute-start | bytes 786440 | tf_op jit(solution)/shard_map/ppermute | solution.py:176
  28.2 5.9 %collective-permute-start.8 = (bf16[16,4096]{1,0:T(8,128)(2,1)S(1)}, bf16[16,4096]{1,0:T(8,128)(2,1)S(1)}, u32[]{:S(2)}, u32[]{:S(2)}) collective-permute-start(bf16[16,4096]{1,0:T(8,128)(2,1)S(1)} %swiglu.1), channel_id=1, source_target_pairs={{0,12},{1,0},{2,4},{3,8},{4,13},{5,1},{6,5},{7,9},{8,14},{9,2},{10... | collective-permute-start | bytes 393224 | tf_op jit(solution)/shard_map/ppermute | solution.py:209
  30.2 8.2 %collective-permute-start.7 = (bf16[16,4096]{1,0:T(8,128)(2,1)S(1)}, bf16[16,4096]{1,0:T(8,128)(2,1)S(1)}, u32[]{:S(2)}, u32[]{:S(2)}) collective-permute-start(bf16[16,4096]{1,0:T(8,128)(2,1)S(1)} %swiglu.1), channel_id=1, source_target_pairs={{0,8},{1,12},{2,0},{3,4},{4,9},{5,13},{6,1},{7,5},{8,10},{9,14},{1... | collective-permute-start | bytes 393224 | tf_op jit(solution)/shard_map/ppermute | solution.py:209
  31.4 7.9 %collective-permute-start.6 = (bf16[16,4096]{1,0:T(8,128)(2,1)S(1)}, bf16[16,4096]{1,0:T(8,128)(2,1)S(1)}, u32[]{:S(2)}, u32[]{:S(2)}) collective-permute-start(bf16[16,4096]{1,0:T(8,128)(2,1)S(1)} %swiglu.1), channel_id=1, source_target_pairs={{0,4},{1,8},{2,12},{3,0},{4,5},{5,9},{6,13},{7,1},{8,6},{9,10},{10... | collective-permute-start | bytes 393224 | tf_op jit(solution)/shard_map/ppermute | solution.py:209
  32.2 7.1 %collective-permute-start.5 = (bf16[16,4096]{1,0:T(8,128)(2,1)S(1)}, bf16[16,4096]{1,0:T(8,128)(2,1)S(1)}, u32[]{:S(2)}, u32[]{:S(2)}) collective-permute-start(bf16[16,4096]{1,0:T(8,128)(2,1)S(1)} %swiglu.1), channel_id=1, source_target_pairs={{0,0},{1,4},{2,8},{3,12},{4,1},{5,5},{6,9},{7,13},{8,2},{9,6},{10,... | collective-permute-start | bytes 393224 | tf_op jit(solution)/shard_map/ppermute | solution.py:209
  42.8 1.4 %collective-permute-start.9 = (bf16[32,2048]{1,0:T(8,128)(2,1)S(1)}, bf16[32,2048]{1,0:T(8,128)(2,1)S(1)}, u32[]{:S(2)}, u32[]{:S(2)}) collective-permute-start(bf16[32,2048]{1,0:T(8,128)(2,1)S(1)} %get-tuple-element.26), channel_id=1, source_target_pairs={{0,1},{1,0},{2,3},{3,2},{4,5},{5,4},{6,7},{7,6},{8,9},{9,8},{10,11... | collective-permute-start | bytes 393224 | tf_op jit(solution)/shard_map/ppermute | solution.py:176
  44.3 8.4 %collective-permute-start.10 = (bf16[16,2048]{1,0:T(8,128)(2,1)S(1)}, bf16[16,2048]{1,0:T(8,128)(2,1)S(1)}, u32[]{:S(2)}, u32[]{:S(2)}) collective-permute-start(bf16[16,2048]{1,0:T(8,128)(2,1)S(1)} %get-tuple-element.28), channel_id=1, source_target_pairs={{0,2},{1,3},{2,0},{3,1},{4,6},{5,7},{6,4},{7,5},{8,10},{9,11},{10,... | collective-permute-start | bytes 196616 | tf_op jit(solution)/shard_map/ppermute | solution.py:176
  (1 other events, 0.8 us)

commit v3 on v2

--- a/solution.py
+++ b/solution.py
@@ -9,11 +9,12 @@
 
 VMEM = pl.BlockSpec(memory_space=pltpu.VMEM)
 SMEM = pl.BlockSpec(memory_space=pltpu.SMEM)
+EARLY = (1, 3)
 
 
 class Panels:
-    def __init__(self, panels, cap, least, step):
-        self.panels, self.cap, self.least = panels, cap, least
+    def __init__(self, first, panels, cap, least, step):
+        self.first, self.panels, self.cap, self.least = first, panels, cap, least
         self.group = math.gcd(panels, 4)
         low, high = max(1, least // 2), cap // 2
         self.sizes = sorted({*range(low, high, step), high})
@@ -25,7 +26,7 @@
         return (pairs - self.low + self.step - 1) // self.step
 
     def fill(self, counts_ref, table_ref):
-        levels = [self.level(counts_ref[h]) for h in range(self.panels)]
+        levels = [self.level(counts_ref[self.first + h]) for h in range(self.panels)]
         kinds = len(self.sizes)
         tally = [sum((lv == k).astype(jnp.int32) for lv in levels) for k in range(kinds)]
         at = [jnp.int32(0)]
@@ -35,7 +36,7 @@
             spot = at[0]
             for k in range(1, kinds):
                 spot = jnp.where(lv == k, at[k], spot)
-            table_ref[spot] = jnp.int32(h)
+            table_ref[spot] = jnp.int32(self.first + h)
             at = [a + (lv == k).astype(jnp.int32) for k, a in enumerate(at)]
         for g in range(self.panels // self.group):
             table_ref[self.panels + g] = self.level(counts_ref[table_ref[(g + 1) * self.group - 1]])
@@ -72,24 +73,28 @@
 
 
 def product(kind, xs, chunk_of, counts, lists, slots_first, table, tiles, name):
-    panels, cap, block, width = tiles.shape
-    rows = sum(x.shape[0] for x in xs)
-    blocks = xs[0].shape[1] // block
+    _, _, block, width = tiles.shape
+    panels, group = kind.panels, kind.group
     pieces = len(xs)
+    rows = sum(lanes[0].shape[0] for lanes in xs)
+    blocks = sum(x.shape[1] for x in xs[0]) // block
     part = rows // 4
-    group = kind.group
 
     def body(counts_ref, lists_ref, table_ref, *rest):
-        x_refs = rest[:pieces]
-        tiles_ref, kept, sent, x_all = rest[pieces:]
+        x_refs = list(rest[:-4])
+        tiles_ref, kept, sent, x_all = rest[-4:]
         col = lax.axis_index("col")
+        grouped = [[x_refs.pop(0) for _ in lanes] for lanes in xs]
         for t in range(4):
             flip = chunk_of(t) ^ col
             spot = (flip & 1) * 2 + flip // 2
             at = pl.ds(pl.multiple_of(spot * part, 16), part)
-            for b in range(blocks):
-                lanes = slice(b * block, (b + 1) * block)
-                x_all[b, at, :] = x_refs[t][:, lanes] if pieces == 4 else x_refs[0][t * part : (t + 1) * part, lanes]
+            lead = slice(0, part) if pieces == 4 else slice(t * part, (t + 1) * part)
+            b = 0
+            for ref in grouped[t if pieces == 4 else 0]:
+                for lo in range(0, ref.shape[1], block):
+                    x_all[b, at, :] = ref[lead, lo : lo + block]
+                    b += 1
 
         @pl.loop(0, panels // group)
         def _(g):
@@ -110,7 +115,7 @@
                         lhs = jnp.concatenate(chosen, axis=1)
                         rhs = tiles_ref[panel, : 2 * pairs].reshape(2 * pairs * block, width)
                         sums = jnp.dot(lhs, rhs, preferred_element_type=jnp.float32)
-                        lanes = pl.ds(pl.multiple_of(panel * width, width), width)
+                        lanes = pl.ds(pl.multiple_of((panel - kind.first) * width, width), width)
                         kept[:, lanes] = sums[: rows // 2]
                         sent[:, lanes] = sums[rows // 2 :].astype(sent.dtype)
 
@@ -120,13 +125,13 @@
             jax.ShapeDtypeStruct((rows // 2, panels * width), jnp.float32),
             jax.ShapeDtypeStruct((rows // 2, panels * width), jnp.bfloat16),
         ],
-        in_specs=[SMEM] * 3 + [VMEM] * (pieces + 1),
+        in_specs=[SMEM] * 3 + [VMEM] * (sum(len(lanes) for lanes in xs) + 1),
         out_specs=[VMEM, VMEM],
         scratch_shapes=[pltpu.VMEM((blocks, rows, block), jnp.bfloat16)],
         compiler_params=pltpu.CompilerParams(vmem_limit_bytes=(4 << 20) + rows * blocks * block * 4 + rows * width * 8),
-        cost_estimate=pl.CostEstimate(flops=2 * rows * tiles.size, transcendentals=0, bytes_accessed=tiles.size * 2),
+        cost_estimate=pl.CostEstimate(flops=2 * rows * panels * tiles[0].size, transcendentals=0, bytes_accessed=panels * tiles[0].size * 2),
         name=name,
-    )(counts, lists, table, *xs, tiles)
+    )(counts, lists, table, *[x for lanes in xs for x in lanes], tiles)
 
 
 def elementwise(body, shapes, name, *args):
@@ -151,18 +156,27 @@
     return elementwise(body, shapes, "add_halves", kept, got)
 
 
-def swiglu(own, got, block):
+def swiglu(own, got, block, ahead=None):
     part, width = own.shape
-    panels = width // (2 * block)
-
-    def body(own_ref, got_ref, out_ref):
-        for h in range(panels):
-            lo = h * 2 * block
+    lead = 0 if ahead is None else ahead.shape[1]
+
+    def body(own_ref, got_ref, *rest):
+        for lo in range(0, width, 2 * block):
             gate = own_ref[:, lo : lo + block] + got_ref[:, lo : lo + block].astype(jnp.float32)
             up = own_ref[:, lo + block : lo + 2 * block] + got_ref[:, lo + block : lo + 2 * block].astype(jnp.float32)
-            out_ref[:, h * block : (h + 1) * block] = (gate / (1.0 + jnp.exp(-gate)) * up).astype(jnp.bfloat16)
-
-    return elementwise(body, [jax.ShapeDtypeStruct((part, width // 2), jnp.bfloat16)], "swiglu", own, got)[0]
+            units = (gate / (1.0 + jnp.exp(-gate)) * up).astype(jnp.bfloat16)
+            if lead:
+                rest[1][:, lo // 2 : lo // 2 + block] = units
+                rest[2][:, lead + lo // 2 : lead + lo // 2 + block] = units
+            else:
+                rest[0][:, lo // 2 : lo // 2 + block] = units
+        if lead:
+            rest[2][:, :lead] = rest[0][...]
+
+    shapes = [jax.ShapeDtypeStruct((part, width // 2), jnp.bfloat16)]
+    if lead:
+        return elementwise(body, shapes + [jax.ShapeDtypeStruct((part, lead + width // 2), jnp.bfloat16)], "swiglu", own, got, ahead)
+    return elementwise(body, shapes, "swiglu", own, got)[0]
 
 
 def last_sum(own, got):
@@ -184,37 +198,48 @@
     part = total // cols
     square = rows == cols
 
-    gate_kind = Panels(gate_tiles.shape[0], gate_tiles.shape[2], 4, 1)
-    down_kind = Panels(down_tiles.shape[0], down_tiles.shape[2], 8, 2)
+    halves = 2 if gate_tiles.shape[0] % 2 == 0 else 1
+    each = gate_tiles.shape[0] // halves
+    gate_kinds = [Panels(i * each, each, gate_tiles.shape[2], 4, 1) for i in range(halves)]
+    down_kind = Panels(0, down_tiles.shape[0], down_tiles.shape[2], 8, 2)
     gate_used, down_used = gate_counts.reshape(-1), down_counts.reshape(-1)
+    slots = jnp.transpose(gate_lists, (2, 1, 0))
 
     def chunk_of(k):
         return lax.rem(lax.axis_index("row") + (rows - k), rows) if square else k
 
     tokens, opened = lax.optimization_barrier((tokens, opening()))
     if square:
-        xs = [tokens] + [lax.ppermute(tokens, "row", [(i, (i + k) % rows) for i in range(rows)]) for k in range(1, rows)]
+        xs = [[tokens]] + [[lax.ppermute(tokens, "row", [(i, (i + k) % rows) for i in range(rows)])] for k in range(1, rows)]
     else:
-        xs = [lax.all_gather(tokens, "row", axis=0, tiled=True)]
-    gate_table, down_table = plan([gate_kind, down_kind], [gate_used, down_used], opened)
-
-    kept, sent = product(
-        gate_kind, xs, chunk_of, gate_used, jnp.transpose(gate_lists, (2, 1, 0)), True, gate_table, gate_tiles[:, 0], "gate_up"
-    )
-    summed, crossing = add_halves(kept, flipped(sent, 1))
-    hidden = swiglu(summed, flipped(crossing, 2), block)
+        xs = [[lax.all_gather(tokens, "row", axis=0, tiled=True)]]
+    *gate_tables, down_table = plan([*gate_kinds, down_kind], [gate_used] * halves + [down_used], opened)
+
+    sums = [
+        product(kind, xs, chunk_of, gate_used, slots, True, table, gate_tiles[:, 0], "gate_up")
+        for kind, table in zip(gate_kinds, gate_tables)
+    ]
+    pairs = []
+    for kept, sent in sums:
+        summed, crossing = add_halves(kept, flipped(sent, 1))
+        pairs.append((summed, flipped(crossing, 2)))
+    hidden = swiglu(*pairs[0], block)
+    if len(pairs) > 1:
+        first = hidden
+        second, hidden = swiglu(*pairs[1], block, first)
 
     if square:
-        hs = [
-            lax.ppermute(
-                hidden, ("row", "col"), [(r * cols + c, ((c + k) % rows) * cols + r) for r in range(rows) for c in range(cols)]
-            )
-            for k in range(cols)
-        ]
+
+        def spread(x, k):
+            there = [(r * cols + c, ((c + k) % rows) * cols + r) for r in range(rows) for c in range(cols)]
+            return lax.ppermute(x, ("row", "col"), there)
+
+        early = EARLY if len(pairs) > 1 else ()
+        hs = [[spread(first, k), spread(second, k)] if k in early else [spread(hidden, k)] for k in range(cols)]
     else:
         every = lax.all_gather(hidden, "row", axis=1, tiled=True).reshape(part, cols, -1)
         every = lax.all_to_all(every, "col", 1, 0, tiled=True)
-        hs = [every.reshape(total, -1)]
+        hs = [[every.reshape(total, -1)]]
     kept, sent = product(down_kind, hs, chunk_of, down_used, down_lists, False, down_table, down_tiles[:, 0], "down")
     summed, crossing = add_halves(kept, flipped(sent, 1))
     return last_sum(summed, flipped(crossing, 2))

time: 53.4 us -> 51.5 us (0.964)
  waiting for transfers between devices: 22.4 us -> 14.4 us
  starting transfers between devices: 18.3 us -> 23.3 us
  Pallas kernels: 11.6 us -> 12.4 us
    ppermute x4 -> x6, waiting for transfers between devices: 12.7 us -> 7.7 us  [flipped(): return lax.ppermute(x, 'col', [(i, i ^ bit) for i in range(4)])]
    ppermute x4 -> x6, starting transfers between devices: 4.67 us -> 9.63 us  [spread(): return lax.ppermute(x, ('row', 'col'), there)]
    ppermute x4 -> x6, waiting for transfers between devices: 6.41 us -> 3.34 us  [spread(): return lax.ppermute(x, ('row', 'col'), there)]
    pallas_call x2 -> x3, Pallas kernels: 8.62 us -> 9.46 us  [product(): pl.pallas_call(body, out_shape=[jax.ShapeDtypeStruct((rows // 2, panels *...]
    ppermute x4 -> x6, starting transfers between devices: 7.55 us -> 7.58 us  [flipped(): return lax.ppermute(x, 'col', [(i, i ^ bit) for i in range(4)])]
  transfers between devices with their start and end apart: 11 -> 15, of which waited for: 8 -> 7; matrix products, arithmetic and copies ran while one was open for 0% -> 0% of each run, Pallas kernels for 4% -> 11%
where the time goes in v3:
time: 51.5 us; the launch traced here: 51.2 us
  starting transfers between devices  23.3 us (45%)
  waiting for transfers between devices  14.4 us (28%)
  Pallas kernels  12.4 us (24%)
  local copies, waits for them, and re-layouts  0.86 us (2%)
    ppermute x6, starting transfers between devices, spread(): return lax.ppermute(x, ('row', 'col'), there)  9.63 us
    pallas_call x3, Pallas kernels, product(): pl.pallas_call(body, out_shape=[jax.ShapeDtypeStruct((rows // 2, panels *...  9.46 us
    ppermute x6, waiting for transfers between devices, flipped(): return lax.ppermute(x, 'col', [(i, i ^ bit) for i in range(4)])  7.7 us
    ppermute x6, starting transfers between devices, flipped(): return lax.ppermute(x, 'col', [(i, i ^ bit) for i in range(4)])  7.58 us
    ppermute x3, starting transfers between devices, local(): lax.ppermute(tokens, 'row', [(i, (i + k) % rows) for i in range(rows)])  6.06 us
    ppermute x6, waiting for transfers between devices, spread(): return lax.ppermute(x, ('row', 'col'), there)  3.34 us
    ppermute x3, waiting for transfers between devices, local(): lax.ppermute(tokens, 'row', [(i, (i + k) % rows) for i in range(rows)])  3.34 us
    pallas_call x1, Pallas kernels, plan(): pl.pallas_call(body, out_shape=[jax.ShapeDtypeStruct((kind.entries,), jnp...  2.08 us
  transfers between devices with their start and end apart: 15, of which 7 were waited for; matrix products, arithmetic and copies ran while one was open for 0% of the time, Pallas kernels for 11%

profile of v3, /device:TPU:0, one launch (start us, length us, event | category | flops | bytes accessed | tf_op | source)
XLA Modules:
  0.0 51.2 jit_solution(12623092229067848589)
XLA Ops:
  0.0 0.8 %copy-done = bf16[16,2048]{1,0:T(8,128)(2,1)S(1)} copy-done((bf16[16,2048]{1,0:T(8,128)(2,1)S(1)}, bf16[16,2048]{1,0:T(8,128)(2,1)}, u32[]{:S(2)}) %copy-start) | copy-done | bytes 65560
  0.8 5.0 %collective-permute-start.2 = (bf16[16,2048]{1,0:T(8,128)(2,1)S(1)}, bf16[16,2048]{1,0:T(8,128)(2,1)S(1)}, u32[]{:S(2)}, u32[]{:S(2)}) collective-permute-start(bf16[16,2048]{1,0:T(8,128)(2,1)S(1)} %copy-done), channel_id=1, source_target_pairs={{0,12},{4,0},{8,4},{12,8},{1,13},{5,1},{9,5},{13,9},{2,14},{6,2},{... | collective-permute-start | bytes 196616 | tf_op jit(solution)/shard_map/ppermute | solution.py:213
  5.9 1.0 %collective-permute-start = (bf16[16,2048]{1,0:T(8,128)(2,1)S(1)}, bf16[16,2048]{1,0:T(8,128)(2,1)S(1)}, u32[]{:S(2)}, u32[]{:S(2)}) collective-permute-start(bf16[16,2048]{1,0:T(8,128)(2,1)S(1)} %copy-done), channel_id=1, source_target_pairs={{0,4},{4,8},{8,12},{12,0},{1,5},{5,9},{9,13},{13,1},{2,6},{6,10},{... | collective-permute-start | bytes 196616 | tf_op jit(solution)/shard_map/ppermute | solution.py:213
  6.9 2.1 %plan.1 = (s32[20]{0:T(128)S(1)}, s32[20]{0:T(128)S(1)}, s32[20]{0:T(128)S(1)}) custom-call(s32[32]{0:T(128)S(1)} %bitcast.14, s32[32]{0:T(128)S(1)} %bitcast.15, s32[16]{0:T(128)S(1)} %bitcast.18, f32[8,128]{1,0:T(8,128)S(1)} %opening.1.refs_3_), custom_call_target="tpu_custom_call" | custom-call | flops 17179869184 | bytes 4096 | tf_op jit(solution)/shard_map/plan/pallas_call | solution.py:64
  9.0 3.3 %collective-permute-done.1.rest_2_ = bf16[16,2048]{1,0:T(8,128)(2,1)S(1)} collective-permute-done((bf16[16,2048]{1,0:T(8,128)(2,1)S(1)}, bf16[16,2048]{1,0:T(8,128)(2,1)S(1)}, u32[]{:S(2)}, u32[]{:S(2)}) %collective-permute-start.1) | collective-permute-done | bytes 65568 | tf_op jit(solution)/shard_map/ppermute | solution.py:213
  12.5 2.8 %gate_up.3 = (f32[32,4096]{1,0:T(8,128)S(1)}, bf16[32,4096]{1,0:T(8,128)(2,1)S(1)}) custom-call(s32[32]{0:T(128)S(1)} %bitcast.16, s32[12,1,32]{2,1,0:T(1,128)S(1)} %bitcast.12, s32[20]{0:T(128)S(1)} %get-tuple-element.32.table_ref, bf16[16,2048]{1,0:T(8,128)(2,1)S(1)} %copy-done, bf16[16,2048]{1,0:T(8,128)(2,1)S(1)} %collective-permute-done.rest_1_, ...), custom_call_target="tpu_custom_call" | custom-call | flops 805306368 | bytes 12582912 | tf_op jit(solution)/shard_map/gate_up/pallas_call | solution.py:122
  15.4 3.3 %gate_up.2 = (f32[32,4096]{1,0:T(8,128)S(1)}, bf16[32,4096]{1,0:T(8,128)(2,1)S(1)}) custom-call(s32[32]{0:T(128)S(1)} %bitcast.17, s32[12,1,32]{2,1,0:T(1,128)S(1)} %bitcast.13, s32[20]{0:T(128)S(1)} %get-tuple-element.26.table_ref, bf16[16,2048]{1,0:T(8,128)(2,1)S(1)} %copy-done, bf16[16,2048]{1,0:T(8,128)(2,1)S(1)} %collective-permute-done.rest_1_, ...), custom_call_target="tpu_custom_call" | custom-call | flops 805306368 | bytes 12582912 | tf_op jit(solution)/shard_map/gate_up/pallas_call | solution.py:122
  18.7 0.4 collective-permute-start.3
  19.1 1.6 %collective-permute-start.6 = (bf16[16,4096]{1,0:T(8,128)(2,1)S(1)}, bf16[16,4096]{1,0:T(8,128)(2,1)S(1)}, u32[]{:S(2)}, u32[]{:S(2)}) collective-permute-start(bf16[16,4096]{1,0:T(8,128)(2,1)S(1)} %get-tuple-element.36), channel_id=1, source_target_pairs={{0,2},{1,3},{2,0},{3,1},{4,6},{5,7},{6,4},{7,5},{8,10},{9,11},{10,... | collective-permute-start | bytes 393224 | tf_op jit(solution)/shard_map/ppermute | solution.py:190
  20.7 1.1 %collective-permute-start.4 = (bf16[16,4096]{1,0:T(8,128)(2,1)S(1)}, bf16[16,4096]{1,0:T(8,128)(2,1)S(1)}, u32[]{:S(2)}, u32[]{:S(2)}) collective-permute-start(bf16[16,4096]{1,0:T(8,128)(2,1)S(1)} %get-tuple-element.31), channel_id=1, source_target_pairs={{0,2},{1,3},{2,0},{3,1},{4,6},{5,7},{6,4},{7,5},{8,10},{9,11},{10,... | collective-permute-start | bytes 393224 | tf_op jit(solution)/shard_map/ppermute | solution.py:190
  21.9 3.7 %collective-permute-done.6.got_ref = bf16[16,4096]{1,0:T(8,128)(2,1)S(1)} collective-permute-done((bf16[16,4096]{1,0:T(8,128)(2,1)S(1)}, bf16[16,4096]{1,0:T(8,128)(2,1)S(1)}, u32[]{:S(2)}, u32[]{:S(2)}) %collective-permute-start.6) | collective-permute-done | bytes 131104 | tf_op jit(solution)/shard_map/ppermute | solution.py:190
  25.6 1.7 %collective-permute-start.11 = (bf16[16,2048]{1,0:T(8,128)(2,1)S(1)}, bf16[16,2048]{1,0:T(8,128)(2,1)S(1)}, u32[]{:S(2)}, u32[]{:S(2)}) collective-permute-start(bf16[16,2048]{1,0:T(8,128)(2,1)S(1)} %swiglu.2.rest_0_), channel_id=1, source_target_pairs={{0,12},{1,0},{2,4},{3,8},{4,13},{5,1},{6,5},{7,9},{8,14},{9,2},{10... | collective-permute-start | bytes 196616 | tf_op jit(solution)/shard_map/ppermute | solution.py:235
  27.7 1.5 %collective-permute-start.10 = (bf16[16,4096]{1,0:T(8,128)(2,1)S(1)}, bf16[16,4096]{1,0:T(8,128)(2,1)S(1)}, u32[]{:S(2)}, u32[]{:S(2)}) collective-permute-start(bf16[16,4096]{1,0:T(8,128)(2,1)S(1)} %get-tuple-element.37), channel_id=1, source_target_pairs={{0,8},{1,12},{2,0},{3,4},{4,9},{5,13},{6,1},{7,5},{8,10},{9,14},{1... | collective-permute-start | bytes 393224 | tf_op jit(solution)/shard_map/ppermute | solution.py:235
  29.1 0.7 %collective-permute-start.7 = (bf16[16,4096]{1,0:T(8,128)(2,1)S(1)}, bf16[16,4096]{1,0:T(8,128)(2,1)S(1)}, u32[]{:S(2)}, u32[]{:S(2)}) collective-permute-start(bf16[16,4096]{1,0:T(8,128)(2,1)S(1)} %get-tuple-element.37), channel_id=1, source_target_pairs={{0,0},{1,4},{2,8},{3,12},{4,1},{5,5},{6,9},{7,13},{8,2},{9,6},{10,... | collective-permute-start | bytes 393224 | tf_op jit(solution)/shard_map/ppermute | solution.py:235
  29.8 3.2 %collective-permute-start.8 = (bf16[16,2048]{1,0:T(8,128)(2,1)S(1)}, bf16[16,2048]{1,0:T(8,128)(2,1)S(1)}, u32[]{:S(2)}, u32[]{:S(2)}) collective-permute-start(bf16[16,2048]{1,0:T(8,128)(2,1)S(1)} %swiglu.2.rest_0_), channel_id=1, source_target_pairs={{0,4},{1,8},{2,12},{3,0},{4,5},{5,9},{6,13},{7,1},{8,6},{9,10},{10... | collective-permute-start | bytes 196616 | tf_op jit(solution)/shard_map/ppermute | solution.py:235
  33.0 1.9 %collective-permute-start.12 = (bf16[16,2048]{1,0:T(8,128)(2,1)S(1)}, bf16[16,2048]{1,0:T(8,128)(2,1)S(1)}, u32[]{:S(2)}, u32[]{:S(2)}) collective-permute-start(bf16[16,2048]{1,0:T(8,128)(2,1)S(1)} %get-tuple-element.38), channel_id=1, source_target_pairs={{0,12},{1,0},{2,4},{3,8},{4,13},{5,1},{6,5},{7,9},{8,14},{9,2},{10... | collective-permute-start | bytes 196616 | tf_op jit(solution)/shard_map/ppermute | solution.py:235
  34.9 0.8 %collective-permute-start.9 = (bf16[16,2048]{1,0:T(8,128)(2,1)S(1)}, bf16[16,2048]{1,0:T(8,128)(2,1)S(1)}, u32[]{:S(2)}, u32[]{:S(2)}) collective-permute-start(bf16[16,2048]{1,0:T(8,128)(2,1)S(1)} %get-tuple-element.38), channel_id=1, source_target_pairs={{0,4},{1,8},{2,12},{3,0},{4,5},{5,9},{6,13},{7,1},{8,6},{9,10},{10... | collective-permute-start | bytes 196616 | tf_op jit(solution)/shard_map/ppermute | solution.py:235
  35.6 1.7 %collective-permute-done.12.rest_5_ = bf16[16,2048]{1,0:T(8,128)(2,1)S(1)} collective-permute-done((bf16[16,2048]{1,0:T(8,128)(2,1)S(1)}, bf16[16,2048]{1,0:T(8,128)(2,1)S(1)}, u32[]{:S(2)}, u32[]{:S(2)}) %collective-permute-start.12) | collective-permute-done | bytes 65568 | tf_op jit(solution)/shard_map/ppermute | solution.py:235
  37.3 1.6 %collective-permute-done.9.rest_2_ = bf16[16,2048]{1,0:T(8,128)(2,1)S(1)} collective-permute-done((bf16[16,2048]{1,0:T(8,128)(2,1)S(1)}, bf16[16,2048]{1,0:T(8,128)(2,1)S(1)}, u32[]{:S(2)}, u32[]{:S(2)}) %collective-permute-start.9) | collective-permute-done | bytes 65568 | tf_op jit(solution)/shard_map/ppermute | solution.py:235
  39.0 3.3 %down.1 = (f32[32,2048]{1,0:T(8,128)S(1)}, bf16[32,2048]{1,0:T(8,128)(2,1)S(1)}) custom-call(s32[16]{0:T(128)S(1)} %bitcast.19, s32[16,1,24]{2,1,0:T(1,128)S(1)} %copy-done.2, s32[20]{0:T(128)S(1)} %get-tuple-element.25.table_ref, bf16[16,4096]{1,0:T(8,128)(2,1)S(1)} %collective-permute-done.7.rest_0_, bf16[16,2048]{1,0:T(8,128)(2,1)S(1)} %collective-permute-done.8.rest_1_, ...), custom_call_target="tpu_custom_call" | custom-call | flops 805306368 | bytes 12582912 | tf_op jit(solution)/shard_map/down/pallas_call | solution.py:122
  42.5 1.3 %collective-permute-done.13.got_ref = bf16[32,2048]{1,0:T(8,128)(2,1)S(1)} collective-permute-done((bf16[32,2048]{1,0:T(8,128)(2,1)S(1)}, bf16[32,2048]{1,0:T(8,128)(2,1)S(1)}, u32[]{:S(2)}, u32[]{:S(2)}) %collective-permute-start.13) | collective-permute-done | bytes 131104 | tf_op jit(solution)/shard_map/ppermute | solution.py:190
  43.8 4.4 %collective-permute-start.14 = (bf16[16,2048]{1,0:T(8,128)(2,1)S(1)}, bf16[16,2048]{1,0:T(8,128)(2,1)S(1)}, u32[]{:S(2)}, u32[]{:S(2)}) collective-permute-start(bf16[16,2048]{1,0:T(8,128)(2,1)S(1)} %get-tuple-element.42), channel_id=1, source_target_pairs={{0,2},{1,3},{2,0},{3,1},{4,6},{5,7},{6,4},{7,5},{8,10},{9,11},{10,... | collective-permute-start | bytes 196616 | tf_op jit(solution)/shard_map/ppermute | solution.py:190
  48.1 2.4 %collective-permute-done.14.got_ref = bf16[16,2048]{1,0:T(8,128)(2,1)S(1)} collective-permute-done((bf16[16,2048]{1,0:T(8,128)(2,1)S(1)}, bf16[16,2048]{1,0:T(8,128)(2,1)S(1)}, u32[]{:S(2)}, u32[]{:S(2)}) %collective-permute-start.14) | collective-permute-done | bytes 65568 | tf_op jit(solution)/shard_map/ppermute | solution.py:190
  50.5 0.6 %last_sum.1 = bf16[16,2048]{1,0:T(8,128)(2,1)} custom-call(f32[16,2048]{1,0:T(8,128)S(1)} %get-tuple-element.41.own_ref, bf16[16,2048]{1,0:T(8,128)(2,1)S(1)} %collective-permute-done.14.got_ref), custom_call_target="tpu_custom_call" | custom-call | tf_op jit(solution)/shard_map/last_sum/pallas_call | solution.py:138
  (47 shorter events, 0.9 us)
Async XLA Ops:
  0.0 6.9 %copy-start.3 = (s32[32,1]{0,1:T(1,128)S(1)}, s32[32,1]{0,1:T(1,128)}, u32[]{:S(2)}) copy-start(s32[32,1]{0,1:T(1,128)} %param.10) | copy-start | bytes 388
  0.0 12.4 %slice-start = ((s8[25165824]{0:T(1024)(128)(4,1)}), s8[4194304]{0:T(1024)(128)(4,1)S(1)}, s32[]{:S(2)}) async-start(s8[25165824]{0:T(1024)(128)(4,1)} %bitcast.5), calls=%async_computation | async-start | bytes 8388608
  0.0 12.4 %slice-start.1 = ((s8[25165824]{0:T(1024)(128)(4,1)}), s8[4194304]{0:T(1024)(128)(4,1)S(1)}, s32[]{:S(2)}) async-start(s8[25165824]{0:T(1024)(128)(4,1)} %bitcast.5), calls=%async_computation.1 | async-start | bytes 8388608
  0.0 12.4 %slice-start.2 = ((s8[25165824]{0:T(1024)(128)(4,1)}), s8[4194304]{0:T(1024)(128)(4,1)S(1)}, s32[]{:S(2)}) async-start(s8[25165824]{0:T(1024)(128)(4,1)} %bitcast.5), calls=%async_computation.2 | async-start | bytes 8388608
  0.0 12.4 %slice-start.3 = ((s8[25165824]{0:T(1024)(128)(4,1)}), s8[4194304]{0:T(1024)(128)(4,1)S(1)}, s32[]{:S(2)}) async-start(s8[25165824]{0:T(1024)(128)(4,1)} %bitcast.5), calls=%async_computation.3 | async-start | bytes 8388608
  0.8 8.2 %collective-permute-start.2 = (bf16[16,2048]{1,0:T(8,128)(2,1)S(1)}, bf16[16,2048]{1,0:T(8,128)(2,1)S(1)}, u32[]{:S(2)}, u32[]{:S(2)}) collective-permute-start(bf16[16,2048]{1,0:T(8,128)(2,1)S(1)} %copy-done), channel_id=1, source_target_pairs={{0,12},{4,0},{8,4},{12,8},{1,13},{5,1},{9,5},{13,9},{2,14},{6,2},{... | collective-permute-start | bytes 196616 | tf_op jit(solution)/shard_map/ppermute | solution.py:213
  5.9 6.5 %collective-permute-start.1 = (bf16[16,2048]{1,0:T(8,128)(2,1)S(1)}, bf16[16,2048]{1,0:T(8,128)(2,1)S(1)}, u32[]{:S(2)}, u32[]{:S(2)}) collective-permute-start(bf16[16,2048]{1,0:T(8,128)(2,1)S(1)} %copy-done), channel_id=1, source_target_pairs={{0,8},{4,12},{8,0},{12,4},{1,9},{5,13},{9,1},{13,5},{2,10},{6,14},... | collective-permute-start | bytes 196616 | tf_op jit(solution)/shard_map/ppermute | solution.py:213
  5.9 6.5 %collective-permute-start = (bf16[16,2048]{1,0:T(8,128)(2,1)S(1)}, bf16[16,2048]{1,0:T(8,128)(2,1)S(1)}, u32[]{:S(2)}, u32[]{:S(2)}) collective-permute-start(bf16[16,2048]{1,0:T(8,128)(2,1)S(1)} %copy-done), channel_id=1, source_target_pairs={{0,4},{4,8},{8,12},{12,0},{1,5},{5,9},{9,13},{13,1},{2,6},{6,10},{... | collective-permute-start | bytes 196616 | tf_op jit(solution)/shard_map/ppermute | solution.py:213
  12.4 26.5 %slice-start.6 = ((s8[12582912]{0:T(1024)(128)(4,1)}), s8[4194304]{0:T(1024)(128)(4,1)S(1)}, s32[]{:S(2)}) async-start(s8[12582912]{0:T(1024)(128)(4,1)} %bitcast.9), calls=%async_computation.6 | async-start | bytes 8388608
  12.4 26.5 %slice-start.7 = ((s8[12582912]{0:T(1024)(128)(4,1)}), s8[4194304]{0:T(1024)(128)(4,1)S(1)}, s32[]{:S(2)}) async-start(s8[12582912]{0:T(1024)(128)(4,1)} %bitcast.9), calls=%async_computation.7 | async-start | bytes 8388608
  12.5 26.5 %copy-start.2 = (s32[16,1,24]{2,1,0:T(1,128)S(1)}, s32[16,1,24]{2,1,0:T(1,128)}, u32[]{:S(2)}) copy-start(s32[16,1,24]{2,1,0:T(1,128)} %lists_ref.1) | copy-start | bytes 4612
  15.3 3.8 %collective-permute-start.5 = (bf16[32,4096]{1,0:T(8,128)(2,1)S(1)}, bf16[32,4096]{1,0:T(8,128)(2,1)S(1)}, u32[]{:S(2)}, u32[]{:S(2)}) collective-permute-start(bf16[32,4096]{1,0:T(8,128)(2,1)S(1)} %get-tuple-element.34), channel_id=1, source_target_pairs={{0,1},{1,0},{2,3},{3,2},{4,5},{5,4},{6,7},{7,6},{8,9},{9,8},{10,11... | collective-permute-start | bytes 786440 | tf_op jit(solution)/shard_map/ppermute | solution.py:190
  15.4 23.6 %slice-start.8 = ((s8[12582912]{0:T(1024)(128)(4,1)}), s8[4194304]{0:T(1024)(128)(4,1)S(1)}, s32[]{:S(2)}) async-start(s8[12582912]{0:T(1024)(128)(4,1)} %bitcast.9), calls=%async_computation.8 | async-start | bytes 8388608
  18.7 2.0 %collective-permute-start.3 = (bf16[32,4096]{1,0:T(8,128)(2,1)S(1)}, bf16[32,4096]{1,0:T(8,128)(2,1)S(1)}, u32[]{:S(2)}, u32[]{:S(2)}) collective-permute-start(bf16[32,4096]{1,0:T(8,128)(2,1)S(1)} %get-tuple-element.29), channel_id=1, source_target_pairs={{0,1},{1,0},{2,3},{3,2},{4,5},{5,4},{6,7},{7,6},{8,9},{9,8},{10,11... | collective-permute-start | bytes 786440 | tf_op jit(solution)/shard_map/ppermute | solution.py:190
  19.1 6.4 %collective-permute-start.6 = (bf16[16,4096]{1,0:T(8,128)(2,1)S(1)}, bf16[16,4096]{1,0:T(8,128)(2,1)S(1)}, u32[]{:S(2)}, u32[]{:S(2)}) collective-permute-start(bf16[16,4096]{1,0:T(8,128)(2,1)S(1)} %get-tuple-element.36), channel_id=1, source_target_pairs={{0,2},{1,3},{2,0},{3,1},{4,6},{5,7},{6,4},{7,5},{8,10},{9,11},{10,... | collective-permute-start | bytes 393224 | tf_op jit(solution)/shard_map/ppermute | solution.py:190
  20.7 6.9 %collective-permute-start.4 = (bf16[16,4096]{1,0:T(8,128)(2,1)S(1)}, bf16[16,4096]{1,0:T(8,128)(2,1)S(1)}, u32[]{:S(2)}, u32[]{:S(2)}) collective-permute-start(bf16[16,4096]{1,0:T(8,128)(2,1)S(1)} %get-tuple-element.31), channel_id=1, source_target_pairs={{0,2},{1,3},{2,0},{3,1},{4,6},{5,7},{6,4},{7,5},{8,10},{9,11},{10,... | collective-permute-start | bytes 393224 | tf_op jit(solution)/shard_map/ppermute | solution.py:190
  25.6 9.3 %collective-permute-start.11 = (bf16[16,2048]{1,0:T(8,128)(2,1)S(1)}, bf16[16,2048]{1,0:T(8,128)(2,1)S(1)}, u32[]{:S(2)}, u32[]{:S(2)}) collective-permute-start(bf16[16,2048]{1,0:T(8,128)(2,1)S(1)} %swiglu.2.rest_0_), channel_id=1, source_target_pairs={{0,12},{1,0},{2,4},{3,8},{4,13},{5,1},{6,5},{7,9},{8,14},{9,2},{10... | collective-permute-start | bytes 196616 | tf_op jit(solution)/shard_map/ppermute | solution.py:235
  27.7 11.3 %collective-permute-start.10 = (bf16[16,4096]{1,0:T(8,128)(2,1)S(1)}, bf16[16,4096]{1,0:T(8,128)(2,1)S(1)}, u32[]{:S(2)}, u32[]{:S(2)}) collective-permute-start(bf16[16,4096]{1,0:T(8,128)(2,1)S(1)} %get-tuple-element.37), channel_id=1, source_target_pairs={{0,8},{1,12},{2,0},{3,4},{4,9},{5,13},{6,1},{7,5},{8,10},{9,14},{1... | collective-permute-start | bytes 393224 | tf_op jit(solution)/shard_map/ppermute | solution.py:235
  29.1 9.8 %collective-permute-start.7 = (bf16[16,4096]{1,0:T(8,128)(2,1)S(1)}, bf16[16,4096]{1,0:T(8,128)(2,1)S(1)}, u32[]{:S(2)}, u32[]{:S(2)}) collective-permute-start(bf16[16,4096]{1,0:T(8,128)(2,1)S(1)} %get-tuple-element.37), channel_id=1, source_target_pairs={{0,0},{1,4},{2,8},{3,12},{4,1},{5,5},{6,9},{7,13},{8,2},{9,6},{10,... | collective-permute-start | bytes 393224 | tf_op jit(solution)/shard_map/ppermute | solution.py:235
  29.8 5.8 %collective-permute-start.8 = (bf16[16,2048]{1,0:T(8,128)(2,1)S(1)}, bf16[16,2048]{1,0:T(8,128)(2,1)S(1)}, u32[]{:S(2)}, u32[]{:S(2)}) collective-permute-start(bf16[16,2048]{1,0:T(8,128)(2,1)S(1)} %swiglu.2.rest_0_), channel_id=1, source_target_pairs={{0,4},{1,8},{2,12},{3,0},{4,5},{5,9},{6,13},{7,1},{8,6},{9,10},{10... | collective-permute-start | bytes 196616 | tf_op jit(solution)/shard_map/ppermute | solution.py:235
  33.0 4.3 %collective-permute-start.12 = (bf16[16,2048]{1,0:T(8,128)(2,1)S(1)}, bf16[16,2048]{1,0:T(8,128)(2,1)S(1)}, u32[]{:S(2)}, u32[]{:S(2)}) collective-permute-start(bf16[16,2048]{1,0:T(8,128)(2,1)S(1)} %get-tuple-element.38), channel_id=1, source_target_pairs={{0,12},{1,0},{2,4},{3,8},{4,13},{5,1},{6,5},{7,9},{8,14},{9,2},{10... | collective-permute-start | bytes 196616 | tf_op jit(solution)/shard_map/ppermute | solution.py:235
  34.9 4.1 %collective-permute-start.9 = (bf16[16,2048]{1,0:T(8,128)(2,1)S(1)}, bf16[16,2048]{1,0:T(8,128)(2,1)S(1)}, u32[]{:S(2)}, u32[]{:S(2)}) collective-permute-start(bf16[16,2048]{1,0:T(8,128)(2,1)S(1)} %get-tuple-element.38), channel_id=1, source_target_pairs={{0,4},{1,8},{2,12},{3,0},{4,5},{5,9},{6,13},{7,1},{8,6},{9,10},{10... | collective-permute-start | bytes 196616 | tf_op jit(solution)/shard_map/ppermute | solution.py:235
  42.3 1.4 %collective-permute-start.13 = (bf16[32,2048]{1,0:T(8,128)(2,1)S(1)}, bf16[32,2048]{1,0:T(8,128)(2,1)S(1)}, u32[]{:S(2)}, u32[]{:S(2)}) collective-permute-start(bf16[32,2048]{1,0:T(8,128)(2,1)S(1)} %get-tuple-element.40), channel_id=1, source_target_pairs={{0,1},{1,0},{2,3},{3,2},{4,5},{5,4},{6,7},{7,6},{8,9},{9,8},{10,11... | collective-permute-start | bytes 393224 | tf_op jit(solution)/shard_map/ppermute | solution.py:190
  43.8 6.8 %collective-permute-start.14 = (bf16[16,2048]{1,0:T(8,128)(2,1)S(1)}, bf16[16,2048]{1,0:T(8,128)(2,1)S(1)}, u32[]{:S(2)}, u32[]{:S(2)}) collective-permute-start(bf16[16,2048]{1,0:T(8,128)(2,1)S(1)} %get-tuple-element.42), channel_id=1, source_target_pairs={{0,2},{1,3},{2,0},{3,1},{4,6},{5,7},{6,4},{7,5},{8,10},{9,11},{10,... | collective-permute-start | bytes 196616 | tf_op jit(solution)/shard_map/ppermute | solution.py:190
  (5 other events, 24.2 us)

commit v4 on v3

--- a/solution.py
+++ b/solution.py
@@ -66,13 +66,13 @@
         out_shape=[jax.ShapeDtypeStruct((kind.entries,), jnp.int32) for kind in kinds],
         in_specs=[SMEM] * len(kinds) + [VMEM],
         out_specs=[SMEM] * len(kinds),
-        cost_estimate=pl.CostEstimate(flops=1 << 34, transcendentals=0, bytes_accessed=4096),
+        cost_estimate=pl.CostEstimate(flops=1 << 10, transcendentals=0, bytes_accessed=4096),
         compiler_params=pltpu.CompilerParams(vmem_limit_bytes=1 << 20),
         name="plan",
     )(*counts, after)
 
 
-def product(kind, xs, chunk_of, counts, lists, slots_first, table, tiles, name):
+def product(kind, xs, chunk_of, counts, lists, slots_first, table, tiles, name, outs):
     _, _, block, width = tiles.shape
     panels, group = kind.panels, kind.group
     pieces = len(xs)
@@ -81,8 +81,9 @@
     part = rows // 4
 
     def body(counts_ref, lists_ref, table_ref, *rest):
-        x_refs = list(rest[:-4])
-        tiles_ref, kept, sent, x_all = rest[-4:]
+        x_refs = list(rest[: -2 - len(outs)])
+        tiles_ref, x_all = rest[-2 - len(outs)], rest[-1]
+        out_refs = rest[-1 - len(outs) : -1]
         col = lax.axis_index("col")
         grouped = [[x_refs.pop(0) for _ in lanes] for lanes in xs]
         for t in range(4):
@@ -116,17 +117,17 @@
                         rhs = tiles_ref[panel, : 2 * pairs].reshape(2 * pairs * block, width)
                         sums = jnp.dot(lhs, rhs, preferred_element_type=jnp.float32)
                         lanes = pl.ds(pl.multiple_of((panel - kind.first) * width, width), width)
-                        kept[:, lanes] = sums[: rows // 2]
-                        sent[:, lanes] = sums[rows // 2 :].astype(sent.dtype)
-
-    return pl.pallas_call(
-        body,
-        out_shape=[
-            jax.ShapeDtypeStruct((rows // 2, panels * width), jnp.float32),
-            jax.ShapeDtypeStruct((rows // 2, panels * width), jnp.bfloat16),
-        ],
+                        at = 0
+                        for out_ref in out_refs:
+                            size = out_ref.shape[0]
+                            out_ref[:, lanes] = sums[at : at + size].astype(out_ref.dtype)
+                            at += size
+
+    return pl.pallas_call(
+        body,
+        out_shape=[jax.ShapeDtypeStruct((n * part, panels * width), dtype) for n, dtype in outs],
         in_specs=[SMEM] * 3 + [VMEM] * (sum(len(lanes) for lanes in xs) + 1),
-        out_specs=[VMEM, VMEM],
+        out_specs=[VMEM] * len(outs),
         scratch_shapes=[pltpu.VMEM((blocks, rows, block), jnp.bfloat16)],
         compiler_params=pltpu.CompilerParams(vmem_limit_bytes=(4 << 20) + rows * blocks * block * 4 + rows * width * 8),
         cost_estimate=pl.CostEstimate(flops=2 * rows * panels * tiles[0].size, transcendentals=0, bytes_accessed=panels * tiles[0].size * 2),
@@ -179,11 +180,14 @@
     return elementwise(body, shapes, "swiglu", own, got)[0]
 
 
-def last_sum(own, got):
-    def body(own_ref, got_ref, out_ref):
-        out_ref[...] = (own_ref[...] + got_ref[...].astype(jnp.float32)).astype(jnp.bfloat16)
-
-    return elementwise(body, [jax.ShapeDtypeStruct(own.shape, jnp.bfloat16)], "last_sum", own, got)[0]
+def last_sum(own, *got):
+    def body(own_ref, *rest):
+        total = own_ref[...]
+        for got_ref in rest[:-1]:
+            total = total + got_ref[...].astype(jnp.float32)
+        rest[-1][...] = total.astype(jnp.bfloat16)
+
+    return elementwise(body, [jax.ShapeDtypeStruct(own.shape, jnp.bfloat16)], "last_sum", own, *got)[0]
 
 
 def flipped(x, bit):
@@ -215,8 +219,9 @@
         xs = [[lax.all_gather(tokens, "row", axis=0, tiled=True)]]
     *gate_tables, down_table = plan([*gate_kinds, down_kind], [gate_used] * halves + [down_used], opened)
 
+    pairwise = [(2, jnp.float32), (2, jnp.bfloat16)]
     sums = [
-        product(kind, xs, chunk_of, gate_used, slots, True, table, gate_tiles[:, 0], "gate_up")
+        product(kind, xs, chunk_of, gate_used, slots, True, table, gate_tiles[:, 0], "gate_up", pairwise)
         for kind, table in zip(gate_kinds, gate_tables)
     ]
     pairs = []
@@ -240,9 +245,9 @@
         every = lax.all_gather(hidden, "row", axis=1, tiled=True).reshape(part, cols, -1)
         every = lax.all_to_all(every, "col", 1, 0, tiled=True)
         hs = [[every.reshape(total, -1)]]
-    kept, sent = product(down_kind, hs, chunk_of, down_used, down_lists, False, down_table, down_tiles[:, 0], "down")
-    summed, crossing = add_halves(kept, flipped(sent, 1))
-    return last_sum(summed, flipped(crossing, 2))
+    straight = [(1, jnp.float32)] + [(1, jnp.bfloat16)] * 3
+    own, *away = product(down_kind, hs, chunk_of, down_used, down_lists, False, down_table, down_tiles[:, 0], "down", straight)
+    return last_sum(own, *[flipped(x, bit) for x, bit in zip(away, (2, 1, 3))])
 
 
 def solution(mesh):

time: 51.5 us -> 51.4 us (level)
  starting transfers between devices: 23.3 us -> 24 us
  waiting for transfers between devices: 14.4 us -> 13.8 us
    ppermute x6 -> x7, waiting for transfers between devices: 7.7 us -> 7.21 us  [flipped(): return lax.ppermute(x, 'col', [(i, i ^ bit) for i in range(4)])]
    ppermute x6 -> x7, starting transfers between devices: 7.58 us -> 7.81 us  [flipped(): return lax.ppermute(x, 'col', [(i, i ^ bit) for i in range(4)])]
  transfers between devices with their start and end apart: 15 -> 16, of which waited for: 7 -> 7; matrix products, arithmetic and copies ran while one was open for 0% -> 0% of each run, Pallas kernels for 11% -> 10%
where the time goes in v4:
time: 51.4 us; the launch traced here: 51 us
  starting transfers between devices  24 us (47%)
  waiting for transfers between devices  13.8 us (27%)
  Pallas kernels  12.2 us (24%)
  local copies, waits for them, and re-layouts  0.86 us (2%)
    ppermute x6, starting transfers between devices, spread(): return lax.ppermute(x, ('row', 'col'), there)  10.1 us
    pallas_call x3, Pallas kernels, product(): pl.pallas_call(body, out_shape=[jax.ShapeDtypeStruct((n * part, panels *...  9.26 us
    ppermute x7, starting transfers between devices, flipped(): return lax.ppermute(x, 'col', [(i, i ^ bit) for i in range(4)])  7.81 us
    ppermute x7, waiting for transfers between devices, flipped(): return lax.ppermute(x, 'col', [(i, i ^ bit) for i in range(4)])  7.21 us
    ppermute x3, starting transfers between devices, local(): lax.ppermute(tokens, 'row', [(i, (i + k) % rows) for i in range(rows)])  6.06 us
    ppermute x3, waiting for transfers between devices, local(): lax.ppermute(tokens, 'row', [(i, (i + k) % rows) for i in range(rows)])  3.36 us
    ppermute x6, waiting for transfers between devices, spread(): return lax.ppermute(x, ('row', 'col'), there)  3.21 us
    pallas_call x1, Pallas kernels, plan(): pl.pallas_call(body, out_shape=[jax.ShapeDtypeStruct((kind.entries,), jnp...  2.08 us
  transfers between devices with their start and end apart: 16, of which 7 were waited for; matrix products, arithmetic and copies ran while one was open for 0% of the time, Pallas kernels for 10%

profile of v4, /device:TPU:0, one launch (start us, length us, event | category | flops | bytes accessed | tf_op | source)
XLA Modules:
  0.0 51.0 jit_solution(384849367458617065)
XLA Ops:
  0.0 0.8 %copy-done.1 = bf16[16,2048]{1,0:T(8,128)(2,1)S(1)} copy-done((bf16[16,2048]{1,0:T(8,128)(2,1)S(1)}, bf16[16,2048]{1,0:T(8,128)(2,1)}, u32[]{:S(2)}) %copy-start.1) | copy-done | bytes 65560
  0.8 5.0 %collective-permute-start.2 = (bf16[16,2048]{1,0:T(8,128)(2,1)S(1)}, bf16[16,2048]{1,0:T(8,128)(2,1)S(1)}, u32[]{:S(2)}, u32[]{:S(2)}) collective-permute-start(bf16[16,2048]{1,0:T(8,128)(2,1)S(1)} %copy-done.1), channel_id=1, source_target_pairs={{0,12},{4,0},{8,4},{12,8},{1,13},{5,1},{9,5},{13,9},{2,14},{6,2},{... | collective-permute-start | bytes 196616 | tf_op jit(solution)/shard_map/ppermute | solution.py:217
  5.9 1.0 %collective-permute-start = (bf16[16,2048]{1,0:T(8,128)(2,1)S(1)}, bf16[16,2048]{1,0:T(8,128)(2,1)S(1)}, u32[]{:S(2)}, u32[]{:S(2)}) collective-permute-start(bf16[16,2048]{1,0:T(8,128)(2,1)S(1)} %copy-done.1), channel_id=1, source_target_pairs={{0,4},{4,8},{8,12},{12,0},{1,5},{5,9},{9,13},{13,1},{2,6},{6,10},{... | collective-permute-start | bytes 196616 | tf_op jit(solution)/shard_map/ppermute | solution.py:217
  6.9 2.1 %plan.1 = (s32[20]{0:T(128)S(1)}, s32[20]{0:T(128)S(1)}, s32[20]{0:T(128)S(1)}) custom-call(s32[32]{0:T(128)S(1)} %bitcast.12, s32[32]{0:T(128)S(1)} %bitcast.13, s32[16]{0:T(128)S(1)} %bitcast.16, f32[8,128]{1,0:T(8,128)S(1)} %opening.1.refs_3_), custom_call_target="tpu_custom_call" | custom-call | flops 1024 | bytes 4096 | tf_op jit(solution)/shard_map/plan/pallas_call | solution.py:64
  9.0 3.4 %collective-permute-done.1.rest_2_ = bf16[16,2048]{1,0:T(8,128)(2,1)S(1)} collective-permute-done((bf16[16,2048]{1,0:T(8,128)(2,1)S(1)}, bf16[16,2048]{1,0:T(8,128)(2,1)S(1)}, u32[]{:S(2)}, u32[]{:S(2)}) %collective-permute-start.1) | collective-permute-done | bytes 65568 | tf_op jit(solution)/shard_map/ppermute | solution.py:217
  12.4 2.9 %gate_up.3 = (f32[32,4096]{1,0:T(8,128)S(1)}, bf16[32,4096]{1,0:T(8,128)(2,1)S(1)}) custom-call(s32[32]{0:T(128)S(1)} %bitcast.14, s32[12,1,32]{2,1,0:T(1,128)S(1)} %bitcast.10, s32[20]{0:T(128)S(1)} %get-tuple-element.32.table_ref, bf16[16,2048]{1,0:T(8,128)(2,1)S(1)} %copy-done.1, bf16[16,2048]{1,0:T(8,128)(2,1)S(1)} %collective-permute-done.rest_1_, ...), custom_call_target="tpu_custom_call" | custom-call | flops 805306368 | bytes 12582912 | tf_op jit(solution)/shard_map/gate_up/pallas_call | solution.py:126
  15.4 3.0 %gate_up.2 = (f32[32,4096]{1,0:T(8,128)S(1)}, bf16[32,4096]{1,0:T(8,128)(2,1)S(1)}) custom-call(s32[32]{0:T(128)S(1)} %bitcast.15, s32[12,1,32]{2,1,0:T(1,128)S(1)} %bitcast.11, s32[20]{0:T(128)S(1)} %get-tuple-element.26.table_ref, bf16[16,2048]{1,0:T(8,128)(2,1)S(1)} %copy-done.1, bf16[16,2048]{1,0:T(8,128)(2,1)S(1)} %collective-permute-done.rest_1_, ...), custom_call_target="tpu_custom_call" | custom-call | flops 805306368 | bytes 12582912 | tf_op jit(solution)/shard_map/gate_up/pallas_call | solution.py:126
  18.5 0.5 collective-permute-start.3
  19.0 1.6 %collective-permute-start.6 = (bf16[16,4096]{1,0:T(8,128)(2,1)S(1)}, bf16[16,4096]{1,0:T(8,128)(2,1)S(1)}, u32[]{:S(2)}, u32[]{:S(2)}) collective-permute-start(bf16[16,4096]{1,0:T(8,128)(2,1)S(1)} %get-tuple-element.36), channel_id=1, source_target_pairs={{0,2},{1,3},{2,0},{3,1},{4,6},{5,7},{6,4},{7,5},{8,10},{9,11},{10,... | collective-permute-start | bytes 393224 | tf_op jit(solution)/shard_map/ppermute | solution.py:194
  20.7 1.2 %collective-permute-start.4 = (bf16[16,4096]{1,0:T(8,128)(2,1)S(1)}, bf16[16,4096]{1,0:T(8,128)(2,1)S(1)}, u32[]{:S(2)}, u32[]{:S(2)}) collective-permute-start(bf16[16,4096]{1,0:T(8,128)(2,1)S(1)} %get-tuple-element.31), channel_id=1, source_target_pairs={{0,2},{1,3},{2,0},{3,1},{4,6},{5,7},{6,4},{7,5},{8,10},{9,11},{10,... | collective-permute-start | bytes 393224 | tf_op jit(solution)/shard_map/ppermute | solution.py:194
  21.9 3.5 %collective-permute-done.6.got_ref = bf16[16,4096]{1,0:T(8,128)(2,1)S(1)} collective-permute-done((bf16[16,4096]{1,0:T(8,128)(2,1)S(1)}, bf16[16,4096]{1,0:T(8,128)(2,1)S(1)}, u32[]{:S(2)}, u32[]{:S(2)}) %collective-permute-start.6) | collective-permute-done | bytes 131104 | tf_op jit(solution)/shard_map/ppermute | solution.py:194
  25.5 1.8 %collective-permute-start.11 = (bf16[16,2048]{1,0:T(8,128)(2,1)S(1)}, bf16[16,2048]{1,0:T(8,128)(2,1)S(1)}, u32[]{:S(2)}, u32[]{:S(2)}) collective-permute-start(bf16[16,2048]{1,0:T(8,128)(2,1)S(1)} %swiglu.2.rest_0_), channel_id=1, source_target_pairs={{0,12},{1,0},{2,4},{3,8},{4,13},{5,1},{6,5},{7,9},{8,14},{9,2},{10... | collective-permute-start | bytes 196616 | tf_op jit(solution)/shard_map/ppermute | solution.py:240
  27.4 1.7 %collective-permute-start.10 = (bf16[16,4096]{1,0:T(8,128)(2,1)S(1)}, bf16[16,4096]{1,0:T(8,128)(2,1)S(1)}, u32[]{:S(2)}, u32[]{:S(2)}) collective-permute-start(bf16[16,4096]{1,0:T(8,128)(2,1)S(1)} %get-tuple-element.37), channel_id=1, source_target_pairs={{0,8},{1,12},{2,0},{3,4},{4,9},{5,13},{6,1},{7,5},{8,10},{9,14},{1... | collective-permute-start | bytes 393224 | tf_op jit(solution)/shard_map/ppermute | solution.py:240
  29.2 0.7 %collective-permute-start.7 = (bf16[16,4096]{1,0:T(8,128)(2,1)S(1)}, bf16[16,4096]{1,0:T(8,128)(2,1)S(1)}, u32[]{:S(2)}, u32[]{:S(2)}) collective-permute-start(bf16[16,4096]{1,0:T(8,128)(2,1)S(1)} %get-tuple-element.37), channel_id=1, source_target_pairs={{0,0},{1,4},{2,8},{3,12},{4,1},{5,5},{6,9},{7,13},{8,2},{9,6},{10,... | collective-permute-start | bytes 393224 | tf_op jit(solution)/shard_map/ppermute | solution.py:240
  29.8 3.0 %collective-permute-start.8 = (bf16[16,2048]{1,0:T(8,128)(2,1)S(1)}, bf16[16,2048]{1,0:T(8,128)(2,1)S(1)}, u32[]{:S(2)}, u32[]{:S(2)}) collective-permute-start(bf16[16,2048]{1,0:T(8,128)(2,1)S(1)} %swiglu.2.rest_0_), channel_id=1, source_target_pairs={{0,4},{1,8},{2,12},{3,0},{4,5},{5,9},{6,13},{7,1},{8,6},{9,10},{10... | collective-permute-start | bytes 196616 | tf_op jit(solution)/shard_map/ppermute | solution.py:240
  32.8 2.0 %collective-permute-start.12 = (bf16[16,2048]{1,0:T(8,128)(2,1)S(1)}, bf16[16,2048]{1,0:T(8,128)(2,1)S(1)}, u32[]{:S(2)}, u32[]{:S(2)}) collective-permute-start(bf16[16,2048]{1,0:T(8,128)(2,1)S(1)} %get-tuple-element.38), channel_id=1, source_target_pairs={{0,12},{1,0},{2,4},{3,8},{4,13},{5,1},{6,5},{7,9},{8,14},{9,2},{10... | collective-permute-start | bytes 196616 | tf_op jit(solution)/shard_map/ppermute | solution.py:240
  34.8 1.0 %collective-permute-start.9 = (bf16[16,2048]{1,0:T(8,128)(2,1)S(1)}, bf16[16,2048]{1,0:T(8,128)(2,1)S(1)}, u32[]{:S(2)}, u32[]{:S(2)}) collective-permute-start(bf16[16,2048]{1,0:T(8,128)(2,1)S(1)} %get-tuple-element.38), channel_id=1, source_target_pairs={{0,4},{1,8},{2,12},{3,0},{4,5},{5,9},{6,13},{7,1},{8,6},{9,10},{10... | collective-permute-start | bytes 196616 | tf_op jit(solution)/shard_map/ppermute | solution.py:240
  35.8 1.5 %collective-permute-done.12.rest_5_ = bf16[16,2048]{1,0:T(8,128)(2,1)S(1)} collective-permute-done((bf16[16,2048]{1,0:T(8,128)(2,1)S(1)}, bf16[16,2048]{1,0:T(8,128)(2,1)S(1)}, u32[]{:S(2)}, u32[]{:S(2)}) %collective-permute-start.12) | collective-permute-done | bytes 65568 | tf_op jit(solution)/shard_map/ppermute | solution.py:240
  37.3 1.7 %collective-permute-done.9.rest_2_ = bf16[16,2048]{1,0:T(8,128)(2,1)S(1)} collective-permute-done((bf16[16,2048]{1,0:T(8,128)(2,1)S(1)}, bf16[16,2048]{1,0:T(8,128)(2,1)S(1)}, u32[]{:S(2)}, u32[]{:S(2)}) %collective-permute-start.9) | collective-permute-done | bytes 65568 | tf_op jit(solution)/shard_map/ppermute | solution.py:240
  39.0 3.3 %down.1 = (f32[16,2048]{1,0:T(8,128)S(1)}, bf16[16,2048]{1,0:T(8,128)(2,1)S(1)}, bf16[16,2048]{1,0:T(8,128)(2,1)S(1)}, bf16[16,2048]{1,0:T(8,128)(2,1)S(1)}) custom-call(s32[16]{0:T(128)S(1)} %bitcast.17, s32[16,1,24]{2,1,0:T(1,128)S(1)} %copy-done.3, s32[20]{0:T(128)S(1)} %get-tuple-element.25.table_ref, ...), custom_call_target="tpu_custom_call" | custom-call | flops 805306368 | bytes 12582912 | tf_op jit(solution)/shard_map/down/pallas_call | solution.py:126
  42.3 4.2 %collective-permute-start.13 = (bf16[16,2048]{1,0:T(8,128)(2,1)S(1)}, bf16[16,2048]{1,0:T(8,128)(2,1)S(1)}, u32[]{:S(2)}, u32[]{:S(2)}) collective-permute-start(bf16[16,2048]{1,0:T(8,128)(2,1)S(1)} %get-tuple-element.40), channel_id=1, source_target_pairs={{0,2},{1,3},{2,0},{3,1},{4,6},{5,7},{6,4},{7,5},{8,10},{9,11},{10,... | collective-permute-start | bytes 196616 | tf_op jit(solution)/shard_map/ppermute | solution.py:194
  46.8 2.1 %collective-permute-done.13.rest_0_ = bf16[16,2048]{1,0:T(8,128)(2,1)S(1)} collective-permute-done((bf16[16,2048]{1,0:T(8,128)(2,1)S(1)}, bf16[16,2048]{1,0:T(8,128)(2,1)S(1)}, u32[]{:S(2)}, u32[]{:S(2)}) %collective-permute-start.13) | collective-permute-done | bytes 65568 | tf_op jit(solution)/shard_map/ppermute | solution.py:194
  48.9 1.4 %collective-permute-done.15.rest_2_ = bf16[16,2048]{1,0:T(8,128)(2,1)S(1)} collective-permute-done((bf16[16,2048]{1,0:T(8,128)(2,1)S(1)}, bf16[16,2048]{1,0:T(8,128)(2,1)S(1)}, u32[]{:S(2)}, u32[]{:S(2)}) %collective-permute-start.15) | collective-permute-done | bytes 65568 | tf_op jit(solution)/shard_map/ppermute | solution.py:194
  50.3 0.7 %last_sum.1 = bf16[16,2048]{1,0:T(8,128)(2,1)} custom-call(f32[16,2048]{1,0:T(8,128)S(1)} %get-tuple-element.39.own_ref, bf16[16,2048]{1,0:T(8,128)(2,1)S(1)} %collective-permute-done.13.rest_0_, bf16[16,2048]{1,0:T(8,128)(2,1)S(1)} %collective-permute-done.14.rest_1_, bf16[16,2048]{1,0:T(8,128)(2,1)S(1)} %collective-permute-done.15.rest_2_), custom_call_target="tpu_custom_call" | custom-call | tf_op jit(solution)/shard_map/last_sum/pallas_call | solution.py:139
  (37 shorter events, 0.7 us)
Async XLA Ops:
  0.0 6.9 %copy-start.5 = (s32[16,1]{0,1:T(1,128)S(1)}, s32[16,1]{0,1:T(1,128)}, u32[]{:S(2)}) copy-start(s32[16,1]{0,1:T(1,128)} %param.13) | copy-start | bytes 196
  0.0 6.9 %copy-start.4 = (s32[32,1]{0,1:T(1,128)S(1)}, s32[32,1]{0,1:T(1,128)}, u32[]{:S(2)}) copy-start(s32[32,1]{0,1:T(1,128)} %param.10) | copy-start | bytes 388
  0.0 12.4 %copy-start.2 = (s32[32,1,12]{0,1,2:T(1,128)S(1)}, s32[32,1,12]{0,1,2:T(1,128)}, u32[]{:S(2)}) copy-start(s32[32,1,12]{0,1,2:T(1,128)} %param.9) | copy-start | bytes 4612
  0.0 12.4 %copy-start = (bf16[32,1,12,128,256]{4,3,2,1,0:T(8,128)(2,1)S(1)}, bf16[32,1,12,128,256]{4,3,2,1,0:T(8,128)(2,1)}, u32[]{:S(2)}) copy-start(bf16[32,1,12,128,256]{4,3,2,1,0:T(8,128)(2,1)} %param.8) | copy-start | bytes 75497472
  0.8 8.2 %collective-permute-start.2 = (bf16[16,2048]{1,0:T(8,128)(2,1)S(1)}, bf16[16,2048]{1,0:T(8,128)(2,1)S(1)}, u32[]{:S(2)}, u32[]{:S(2)}) collective-permute-start(bf16[16,2048]{1,0:T(8,128)(2,1)S(1)} %copy-done.1), channel_id=1, source_target_pairs={{0,12},{4,0},{8,4},{12,8},{1,13},{5,1},{9,5},{13,9},{2,14},{6,2},{... | collective-permute-start | bytes 196616 | tf_op jit(solution)/shard_map/ppermute | solution.py:217
  5.9 6.5 %collective-permute-start.1 = (bf16[16,2048]{1,0:T(8,128)(2,1)S(1)}, bf16[16,2048]{1,0:T(8,128)(2,1)S(1)}, u32[]{:S(2)}, u32[]{:S(2)}) collective-permute-start(bf16[16,2048]{1,0:T(8,128)(2,1)S(1)} %copy-done.1), channel_id=1, source_target_pairs={{0,8},{4,12},{8,0},{12,4},{1,9},{5,13},{9,1},{13,5},{2,10},{6,14},... | collective-permute-start | bytes 196616 | tf_op jit(solution)/shard_map/ppermute | solution.py:217
  5.9 6.5 %collective-permute-start = (bf16[16,2048]{1,0:T(8,128)(2,1)S(1)}, bf16[16,2048]{1,0:T(8,128)(2,1)S(1)}, u32[]{:S(2)}, u32[]{:S(2)}) collective-permute-start(bf16[16,2048]{1,0:T(8,128)(2,1)S(1)} %copy-done.1), channel_id=1, source_target_pairs={{0,4},{4,8},{8,12},{12,0},{1,5},{5,9},{9,13},{13,1},{2,6},{6,10},{... | collective-permute-start | bytes 196616 | tf_op jit(solution)/shard_map/ppermute | solution.py:217
  12.4 26.6 %slice-start = ((s8[12582912]{0:T(1024)(128)(4,1)}), s8[4194304]{0:T(1024)(128)(4,1)S(1)}, s32[]{:S(2)}) async-start(s8[12582912]{0:T(1024)(128)(4,1)} %bitcast.7), calls=%async_computation | async-start | bytes 8388608
  12.4 26.6 %slice-start.1 = ((s8[12582912]{0:T(1024)(128)(4,1)}), s8[4194304]{0:T(1024)(128)(4,1)S(1)}, s32[]{:S(2)}) async-start(s8[12582912]{0:T(1024)(128)(4,1)} %bitcast.7), calls=%async_computation.1 | async-start | bytes 8388608
  12.4 26.6 %copy-start.3 = (s32[16,1,24]{2,1,0:T(1,128)S(1)}, s32[16,1,24]{2,1,0:T(1,128)}, u32[]{:S(2)}) copy-start(s32[16,1,24]{2,1,0:T(1,128)} %lists_ref.1) | copy-start | bytes 4612
  15.3 3.6 %collective-permute-start.5 = (bf16[32,4096]{1,0:T(8,128)(2,1)S(1)}, bf16[32,4096]{1,0:T(8,128)(2,1)S(1)}, u32[]{:S(2)}, u32[]{:S(2)}) collective-permute-start(bf16[32,4096]{1,0:T(8,128)(2,1)S(1)} %get-tuple-element.34), channel_id=1, source_target_pairs={{0,1},{1,0},{2,3},{3,2},{4,5},{5,4},{6,7},{7,6},{8,9},{9,8},{10,11... | collective-permute-start | bytes 786440 | tf_op jit(solution)/shard_map/ppermute | solution.py:194
  15.4 23.6 %slice-start.2 = ((s8[12582912]{0:T(1024)(128)(4,1)}), s8[4194304]{0:T(1024)(128)(4,1)S(1)}, s32[]{:S(2)}) async-start(s8[12582912]{0:T(1024)(128)(4,1)} %bitcast.7), calls=%async_computation.2 | async-start | bytes 8388608
  18.5 2.2 %collective-permute-start.3 = (bf16[32,4096]{1,0:T(8,128)(2,1)S(1)}, bf16[32,4096]{1,0:T(8,128)(2,1)S(1)}, u32[]{:S(2)}, u32[]{:S(2)}) collective-permute-start(bf16[32,4096]{1,0:T(8,128)(2,1)S(1)} %get-tuple-element.29), channel_id=1, source_target_pairs={{0,1},{1,0},{2,3},{3,2},{4,5},{5,4},{6,7},{7,6},{8,9},{9,8},{10,11... | collective-permute-start | bytes 786440 | tf_op jit(solution)/shard_map/ppermute | solution.py:194
  19.0 6.4 %collective-permute-start.6 = (bf16[16,4096]{1,0:T(8,128)(2,1)S(1)}, bf16[16,4096]{1,0:T(8,128)(2,1)S(1)}, u32[]{:S(2)}, u32[]{:S(2)}) collective-permute-start(bf16[16,4096]{1,0:T(8,128)(2,1)S(1)} %get-tuple-element.36), channel_id=1, source_target_pairs={{0,2},{1,3},{2,0},{3,1},{4,6},{5,7},{6,4},{7,5},{8,10},{9,11},{10,... | collective-permute-start | bytes 393224 | tf_op jit(solution)/shard_map/ppermute | solution.py:194
  20.7 6.7 %collective-permute-start.4 = (bf16[16,4096]{1,0:T(8,128)(2,1)S(1)}, bf16[16,4096]{1,0:T(8,128)(2,1)S(1)}, u32[]{:S(2)}, u32[]{:S(2)}) collective-permute-start(bf16[16,4096]{1,0:T(8,128)(2,1)S(1)} %get-tuple-element.31), channel_id=1, source_target_pairs={{0,2},{1,3},{2,0},{3,1},{4,6},{5,7},{6,4},{7,5},{8,10},{9,11},{10,... | collective-permute-start | bytes 393224 | tf_op jit(solution)/shard_map/ppermute | solution.py:194
  25.5 9.3 %collective-permute-start.11 = (bf16[16,2048]{1,0:T(8,128)(2,1)S(1)}, bf16[16,2048]{1,0:T(8,128)(2,1)S(1)}, u32[]{:S(2)}, u32[]{:S(2)}) collective-permute-start(bf16[16,2048]{1,0:T(8,128)(2,1)S(1)} %swiglu.2.rest_0_), channel_id=1, source_target_pairs={{0,12},{1,0},{2,4},{3,8},{4,13},{5,1},{6,5},{7,9},{8,14},{9,2},{10... | collective-permute-start | bytes 196616 | tf_op jit(solution)/shard_map/ppermute | solution.py:240
  27.4 11.5 %collective-permute-start.10 = (bf16[16,4096]{1,0:T(8,128)(2,1)S(1)}, bf16[16,4096]{1,0:T(8,128)(2,1)S(1)}, u32[]{:S(2)}, u32[]{:S(2)}) collective-permute-start(bf16[16,4096]{1,0:T(8,128)(2,1)S(1)} %get-tuple-element.37), channel_id=1, source_target_pairs={{0,8},{1,12},{2,0},{3,4},{4,9},{5,13},{6,1},{7,5},{8,10},{9,14},{1... | collective-permute-start | bytes 393224 | tf_op jit(solution)/shard_map/ppermute | solution.py:240
  29.2 9.8 %collective-permute-start.7 = (bf16[16,4096]{1,0:T(8,128)(2,1)S(1)}, bf16[16,4096]{1,0:T(8,128)(2,1)S(1)}, u32[]{:S(2)}, u32[]{:S(2)}) collective-permute-start(bf16[16,4096]{1,0:T(8,128)(2,1)S(1)} %get-tuple-element.37), channel_id=1, source_target_pairs={{0,0},{1,4},{2,8},{3,12},{4,1},{5,5},{6,9},{7,13},{8,2},{9,6},{10,... | collective-permute-start | bytes 393224 | tf_op jit(solution)/shard_map/ppermute | solution.py:240
  29.8 5.9 %collective-permute-start.8 = (bf16[16,2048]{1,0:T(8,128)(2,1)S(1)}, bf16[16,2048]{1,0:T(8,128)(2,1)S(1)}, u32[]{:S(2)}, u32[]{:S(2)}) collective-permute-start(bf16[16,2048]{1,0:T(8,128)(2,1)S(1)} %swiglu.2.rest_0_), channel_id=1, source_target_pairs={{0,4},{1,8},{2,12},{3,0},{4,5},{5,9},{6,13},{7,1},{8,6},{9,10},{10... | collective-permute-start | bytes 196616 | tf_op jit(solution)/shard_map/ppermute | solution.py:240
  32.8 4.5 %collective-permute-start.12 = (bf16[16,2048]{1,0:T(8,128)(2,1)S(1)}, bf16[16,2048]{1,0:T(8,128)(2,1)S(1)}, u32[]{:S(2)}, u32[]{:S(2)}) collective-permute-start(bf16[16,2048]{1,0:T(8,128)(2,1)S(1)} %get-tuple-element.38), channel_id=1, source_target_pairs={{0,12},{1,0},{2,4},{3,8},{4,13},{5,1},{6,5},{7,9},{8,14},{9,2},{10... | collective-permute-start | bytes 196616 | tf_op jit(solution)/shard_map/ppermute | solution.py:240
  34.8 4.2 %collective-permute-start.9 = (bf16[16,2048]{1,0:T(8,128)(2,1)S(1)}, bf16[16,2048]{1,0:T(8,128)(2,1)S(1)}, u32[]{:S(2)}, u32[]{:S(2)}) collective-permute-start(bf16[16,2048]{1,0:T(8,128)(2,1)S(1)} %get-tuple-element.38), channel_id=1, source_target_pairs={{0,4},{1,8},{2,12},{3,0},{4,5},{5,9},{6,13},{7,1},{8,6},{9,10},{10... | collective-permute-start | bytes 196616 | tf_op jit(solution)/shard_map/ppermute | solution.py:240
  42.3 6.6 %collective-permute-start.13 = (bf16[16,2048]{1,0:T(8,128)(2,1)S(1)}, bf16[16,2048]{1,0:T(8,128)(2,1)S(1)}, u32[]{:S(2)}, u32[]{:S(2)}) collective-permute-start(bf16[16,2048]{1,0:T(8,128)(2,1)S(1)} %get-tuple-element.40), channel_id=1, source_target_pairs={{0,2},{1,3},{2,0},{3,1},{4,6},{5,7},{6,4},{7,5},{8,10},{9,11},{10,... | collective-permute-start | bytes 196616 | tf_op jit(solution)/shard_map/ppermute | solution.py:194
  46.6 2.3 %collective-permute-start.14 = (bf16[16,2048]{1,0:T(8,128)(2,1)S(1)}, bf16[16,2048]{1,0:T(8,128)(2,1)S(1)}, u32[]{:S(2)}, u32[]{:S(2)}) collective-permute-start(bf16[16,2048]{1,0:T(8,128)(2,1)S(1)} %get-tuple-element.41), channel_id=1, source_target_pairs={{0,1},{1,0},{2,3},{3,2},{4,5},{5,4},{6,7},{7,6},{8,9},{9,8},{10,11... | collective-permute-start | bytes 196616 | tf_op jit(solution)/shard_map/ppermute | solution.py:194
  46.6 3.7 %collective-permute-start.15 = (bf16[16,2048]{1,0:T(8,128)(2,1)S(1)}, bf16[16,2048]{1,0:T(8,128)(2,1)S(1)}, u32[]{:S(2)}, u32[]{:S(2)}) collective-permute-start(bf16[16,2048]{1,0:T(8,128)(2,1)S(1)} %get-tuple-element.42), channel_id=1, source_target_pairs={{0,3},{1,2},{2,1},{3,0},{4,7},{5,6},{6,5},{7,4},{8,11},{9,10},{10,... | collective-permute-start | bytes 196616 | tf_op jit(solution)/shard_map/ppermute | solution.py:194
  (1 other events, 0.8 us)

commit v5 on v4

--- a/solution.py
+++ b/solution.py
@@ -72,7 +72,7 @@
     )(*counts, after)
 
 
-def product(kind, xs, chunk_of, counts, lists, slots_first, table, tiles, name, outs):
+def product(kind, xs, chunk_of, counts, lists, slots_first, table, tiles, name, outs, ready=None, share=False):
     _, _, block, width = tiles.shape
     panels, group = kind.panels, kind.group
     pieces = len(xs)
@@ -80,10 +80,10 @@
     blocks = sum(x.shape[1] for x in xs[0]) // block
     part = rows // 4
 
-    def body(counts_ref, lists_ref, table_ref, *rest):
-        x_refs = list(rest[: -2 - len(outs)])
-        tiles_ref, x_all = rest[-2 - len(outs)], rest[-1]
-        out_refs = rest[-1 - len(outs) : -1]
+    laid = jax.ShapeDtypeStruct((blocks, rows, block), jnp.bfloat16)
+    operands = [x for lanes in xs for x in lanes] if ready is None else [ready]
+
+    def lay_out(x_refs, x_all):
         col = lax.axis_index("col")
         grouped = [[x_refs.pop(0) for _ in lanes] for lanes in xs]
         for t in range(4):
@@ -96,6 +96,15 @@
                 for lo in range(0, ref.shape[1], block):
                     x_all[b, at, :] = ref[lead, lo : lo + block]
                     b += 1
+
+    def body(counts_ref, lists_ref, table_ref, *rest):
+        if ready is None:
+            x_refs = list(rest[: -2 - len(outs)])
+            tiles_ref, x_all = rest[-2 - len(outs)], rest[-1]
+            out_refs = rest[-1 - len(outs) : -1]
+            lay_out(x_refs, x_all)
+        else:
+            x_all, tiles_ref, *out_refs = rest
 
         @pl.loop(0, panels // group)
         def _(g):
@@ -125,14 +134,14 @@
 
     return pl.pallas_call(
         body,
-        out_shape=[jax.ShapeDtypeStruct((n * part, panels * width), dtype) for n, dtype in outs],
-        in_specs=[SMEM] * 3 + [VMEM] * (sum(len(lanes) for lanes in xs) + 1),
-        out_specs=[VMEM] * len(outs),
-        scratch_shapes=[pltpu.VMEM((blocks, rows, block), jnp.bfloat16)],
+        out_shape=[jax.ShapeDtypeStruct((n * part, panels * width), dtype) for n, dtype in outs] + [laid] * share,
+        in_specs=[SMEM] * 3 + [VMEM] * (len(operands) + 1),
+        out_specs=[VMEM] * (len(outs) + share),
+        scratch_shapes=[] if share or ready is not None else [pltpu.VMEM(laid.shape, laid.dtype)],
         compiler_params=pltpu.CompilerParams(vmem_limit_bytes=(4 << 20) + rows * blocks * block * 4 + rows * width * 8),
         cost_estimate=pl.CostEstimate(flops=2 * rows * panels * tiles[0].size, transcendentals=0, bytes_accessed=panels * tiles[0].size * 2),
         name=name,
-    )(counts, lists, table, *[x for lanes in xs for x in lanes], tiles)
+    )(counts, lists, table, *operands, tiles)
 
 
 def elementwise(body, shapes, name, *args):
@@ -220,10 +229,15 @@
     *gate_tables, down_table = plan([*gate_kinds, down_kind], [gate_used] * halves + [down_used], opened)
 
     pairwise = [(2, jnp.float32), (2, jnp.bfloat16)]
-    sums = [
-        product(kind, xs, chunk_of, gate_used, slots, True, table, gate_tiles[:, 0], "gate_up", pairwise)
-        for kind, table in zip(gate_kinds, gate_tables)
-    ]
+    sums = []
+    laid = None
+    for kind, table in zip(gate_kinds, gate_tables):
+        first = laid is None
+        got = product(
+            kind, xs, chunk_of, gate_used, slots, True, table, gate_tiles[:, 0], "gate_up", pairwise, ready=laid, share=first
+        )
+        sums.append((got[0], got[1]))
+        laid = got[2] if first else laid
     pairs = []
     for kept, sent in sums:
         summed, crossing = add_halves(kept, flipped(sent, 1))

time: 51.4 us -> 51.4 us (level)
  waiting for transfers between devices: 13.8 us -> 14.4 us
where the time goes in v5:
time: 51.4 us; the launch traced here: 51.1 us
  starting transfers between devices  23.6 us (46%)
  waiting for transfers between devices  14.4 us (28%)
  Pallas kernels  12.2 us (24%)
  local copies, waits for them, and re-layouts  0.86 us (2%)
    ppermute x6, starting transfers between devices, spread(): return lax.ppermute(x, ('row', 'col'), there)  10 us
    pallas_call x3, Pallas kernels, product(): pl.pallas_call(body, out_shape=[jax.ShapeDtypeStruct((n * part, panels *...  9.19 us
    ppermute x7, starting transfers between devices, flipped(): return lax.ppermute(x, 'col', [(i, i ^ bit) for i in range(4)])  7.46 us
    ppermute x7, waiting for transfers between devices, flipped(): return lax.ppermute(x, 'col', [(i, i ^ bit) for i in range(4)])  7.38 us
    ppermute x3, starting transfers between devices, local(): lax.ppermute(tokens, 'row', [(i, (i + k) % rows) for i in range(rows)])  6.06 us
    ppermute x6, waiting for transfers between devices, spread(): return lax.ppermute(x, ('row', 'col'), there)  3.64 us
    ppermute x3, waiting for transfers between devices, local(): lax.ppermute(tokens, 'row', [(i, (i + k) % rows) for i in range(rows)])  3.36 us
    pallas_call x1, Pallas kernels, plan(): pl.pallas_call(body, out_shape=[jax.ShapeDtypeStruct((kind.entries,), jnp...  2.08 us
  transfers between devices with their start and end apart: 16, of which 7 were waited for; matrix products, arithmetic and copies ran while one was open for 0% of the time, Pallas kernels for 10%

profile of v5, /device:TPU:0, one launch (start us, length us, event | category | flops | bytes accessed | tf_op | source)
XLA Modules:
  0.0 51.1 jit_solution(2869225777919359650)
XLA Ops:
  0.0 0.8 %copy-done.1 = bf16[16,2048]{1,0:T(8,128)(2,1)S(1)} copy-done((bf16[16,2048]{1,0:T(8,128)(2,1)S(1)}, bf16[16,2048]{1,0:T(8,128)(2,1)}, u32[]{:S(2)}) %copy-start.1) | copy-done | bytes 65560
  0.8 5.0 %collective-permute-start.2 = (bf16[16,2048]{1,0:T(8,128)(2,1)S(1)}, bf16[16,2048]{1,0:T(8,128)(2,1)S(1)}, u32[]{:S(2)}, u32[]{:S(2)}) collective-permute-start(bf16[16,2048]{1,0:T(8,128)(2,1)S(1)} %copy-done.1), channel_id=1, source_target_pairs={{0,12},{4,0},{8,4},{12,8},{1,13},{5,1},{9,5},{13,9},{2,14},{6,2},{... | collective-permute-start | bytes 196616 | tf_op jit(solution)/shard_map/ppermute | solution.py:226
  5.9 1.0 %collective-permute-start = (bf16[16,2048]{1,0:T(8,128)(2,1)S(1)}, bf16[16,2048]{1,0:T(8,128)(2,1)S(1)}, u32[]{:S(2)}, u32[]{:S(2)}) collective-permute-start(bf16[16,2048]{1,0:T(8,128)(2,1)S(1)} %copy-done.1), channel_id=1, source_target_pairs={{0,4},{4,8},{8,12},{12,0},{1,5},{5,9},{9,13},{13,1},{2,6},{6,10},{... | collective-permute-start | bytes 196616 | tf_op jit(solution)/shard_map/ppermute | solution.py:226
  6.9 2.1 %plan.1 = (s32[20]{0:T(128)S(1)}, s32[20]{0:T(128)S(1)}, s32[20]{0:T(128)S(1)}) custom-call(s32[32]{0:T(128)S(1)} %bitcast.12, s32[32]{0:T(128)S(1)} %bitcast.13, s32[16]{0:T(128)S(1)} %bitcast.16, f32[8,128]{1,0:T(8,128)S(1)} %opening.1.refs_3_), custom_call_target="tpu_custom_call" | custom-call | flops 1024 | bytes 4096 | tf_op jit(solution)/shard_map/plan/pallas_call | solution.py:64
  9.0 3.4 %collective-permute-done.1.rest_2_ = bf16[16,2048]{1,0:T(8,128)(2,1)S(1)} collective-permute-done((bf16[16,2048]{1,0:T(8,128)(2,1)S(1)}, bf16[16,2048]{1,0:T(8,128)(2,1)S(1)}, u32[]{:S(2)}, u32[]{:S(2)}) %collective-permute-start.1) | collective-permute-done | bytes 65568 | tf_op jit(solution)/shard_map/ppermute | solution.py:226
  12.4 3.1 %gate_up.2 = (f32[32,4096]{1,0:T(8,128)S(1)}, bf16[32,4096]{1,0:T(8,128)(2,1)S(1)}, bf16[16,64,128]{2,1,0:T(8,128)(2,1)S(1)}) custom-call(s32[32]{0:T(128)S(1)} %bitcast.14, s32[12,1,32]{2,1,0:T(1,128)S(1)} %bitcast.10, s32[20]{0:T(128)S(1)} %get-tuple-element.28.table_ref, bf16[16,2048]{1,0:T(8,128)(2,1)S(1)} %copy-done.1, ...), custom_call_target="tpu_custom_call" | custom-call | flops 805306368 | bytes 12582912 | tf_op jit(solution)/shard_map/gate_up/pallas_call | solution.py:135
  15.6 2.8 %gate_up.3 = (f32[32,4096]{1,0:T(8,128)S(1)}, bf16[32,4096]{1,0:T(8,128)(2,1)S(1)}) custom-call(s32[32]{0:T(128)S(1)} %bitcast.15, s32[12,1,32]{2,1,0:T(1,128)S(1)} %bitcast.11, s32[20]{0:T(128)S(1)} %get-tuple-element.27.table_ref, bf16[16,64,128]{2,1,0:T(8,128)(2,1)S(1)} %get-tuple-element.30.rest_0_, bf16[32,12,128,256]{3,2,1,0:T(8,128)(2,1)S(1)} %bitcast.6), custom_call_target="tpu_custom_call" | custom-call | flops 805306368 | bytes 12582912 | tf_op jit(solution)/shard_map/gate_up/pallas_call | solution.py:135
  18.4 0.5 collective-permute-start.3
  19.0 1.5 %collective-permute-start.6 = (bf16[16,4096]{1,0:T(8,128)(2,1)S(1)}, bf16[16,4096]{1,0:T(8,128)(2,1)S(1)}, u32[]{:S(2)}, u32[]{:S(2)}) collective-permute-start(bf16[16,4096]{1,0:T(8,128)(2,1)S(1)} %get-tuple-element.38), channel_id=1, source_target_pairs={{0,2},{1,3},{2,0},{3,1},{4,6},{5,7},{6,4},{7,5},{8,10},{9,11},{10,... | collective-permute-start | bytes 393224 | tf_op jit(solution)/shard_map/ppermute | solution.py:203
  20.5 1.1 %collective-permute-start.4 = (bf16[16,4096]{1,0:T(8,128)(2,1)S(1)}, bf16[16,4096]{1,0:T(8,128)(2,1)S(1)}, u32[]{:S(2)}, u32[]{:S(2)}) collective-permute-start(bf16[16,4096]{1,0:T(8,128)(2,1)S(1)} %get-tuple-element.34), channel_id=1, source_target_pairs={{0,2},{1,3},{2,0},{3,1},{4,6},{5,7},{6,4},{7,5},{8,10},{9,11},{10,... | collective-permute-start | bytes 393224 | tf_op jit(solution)/shard_map/ppermute | solution.py:203
  21.6 3.8 %collective-permute-done.6.got_ref = bf16[16,4096]{1,0:T(8,128)(2,1)S(1)} collective-permute-done((bf16[16,4096]{1,0:T(8,128)(2,1)S(1)}, bf16[16,4096]{1,0:T(8,128)(2,1)S(1)}, u32[]{:S(2)}, u32[]{:S(2)}) %collective-permute-start.6) | collective-permute-done | bytes 131104 | tf_op jit(solution)/shard_map/ppermute | solution.py:203
  25.4 1.9 %collective-permute-start.11 = (bf16[16,2048]{1,0:T(8,128)(2,1)S(1)}, bf16[16,2048]{1,0:T(8,128)(2,1)S(1)}, u32[]{:S(2)}, u32[]{:S(2)}) collective-permute-start(bf16[16,2048]{1,0:T(8,128)(2,1)S(1)} %swiglu.2.rest_0_), channel_id=1, source_target_pairs={{0,12},{1,0},{2,4},{3,8},{4,13},{5,1},{6,5},{7,9},{8,14},{9,2},{10... | collective-permute-start | bytes 196616 | tf_op jit(solution)/shard_map/ppermute | solution.py:254
  27.4 1.9 %collective-permute-start.10 = (bf16[16,4096]{1,0:T(8,128)(2,1)S(1)}, bf16[16,4096]{1,0:T(8,128)(2,1)S(1)}, u32[]{:S(2)}, u32[]{:S(2)}) collective-permute-start(bf16[16,4096]{1,0:T(8,128)(2,1)S(1)} %get-tuple-element.39), channel_id=1, source_target_pairs={{0,8},{1,12},{2,0},{3,4},{4,9},{5,13},{6,1},{7,5},{8,10},{9,14},{1... | collective-permute-start | bytes 393224 | tf_op jit(solution)/shard_map/ppermute | solution.py:254
  29.3 0.7 %collective-permute-start.7 = (bf16[16,4096]{1,0:T(8,128)(2,1)S(1)}, bf16[16,4096]{1,0:T(8,128)(2,1)S(1)}, u32[]{:S(2)}, u32[]{:S(2)}) collective-permute-start(bf16[16,4096]{1,0:T(8,128)(2,1)S(1)} %get-tuple-element.39), channel_id=1, source_target_pairs={{0,0},{1,4},{2,8},{3,12},{4,1},{5,5},{6,9},{7,13},{8,2},{9,6},{10,... | collective-permute-start | bytes 393224 | tf_op jit(solution)/shard_map/ppermute | solution.py:254
  30.0 3.0 %collective-permute-start.8 = (bf16[16,2048]{1,0:T(8,128)(2,1)S(1)}, bf16[16,2048]{1,0:T(8,128)(2,1)S(1)}, u32[]{:S(2)}, u32[]{:S(2)}) collective-permute-start(bf16[16,2048]{1,0:T(8,128)(2,1)S(1)} %swiglu.2.rest_0_), channel_id=1, source_target_pairs={{0,4},{1,8},{2,12},{3,0},{4,5},{5,9},{6,13},{7,1},{8,6},{9,10},{10... | collective-permute-start | bytes 196616 | tf_op jit(solution)/shard_map/ppermute | solution.py:254
  33.0 2.0 %collective-permute-start.12 = (bf16[16,2048]{1,0:T(8,128)(2,1)S(1)}, bf16[16,2048]{1,0:T(8,128)(2,1)S(1)}, u32[]{:S(2)}, u32[]{:S(2)}) collective-permute-start(bf16[16,2048]{1,0:T(8,128)(2,1)S(1)} %get-tuple-element.40), channel_id=1, source_target_pairs={{0,12},{1,0},{2,4},{3,8},{4,13},{5,1},{6,5},{7,9},{8,14},{9,2},{10... | collective-permute-start | bytes 196616 | tf_op jit(solution)/shard_map/ppermute | solution.py:254
  35.1 0.6 %collective-permute-start.9 = (bf16[16,2048]{1,0:T(8,128)(2,1)S(1)}, bf16[16,2048]{1,0:T(8,128)(2,1)S(1)}, u32[]{:S(2)}, u32[]{:S(2)}) collective-permute-start(bf16[16,2048]{1,0:T(8,128)(2,1)S(1)} %get-tuple-element.40), channel_id=1, source_target_pairs={{0,4},{1,8},{2,12},{3,0},{4,5},{5,9},{6,13},{7,1},{8,6},{9,10},{10... | collective-permute-start | bytes 196616 | tf_op jit(solution)/shard_map/ppermute | solution.py:254
  35.6 1.9 %collective-permute-done.12.rest_5_ = bf16[16,2048]{1,0:T(8,128)(2,1)S(1)} collective-permute-done((bf16[16,2048]{1,0:T(8,128)(2,1)S(1)}, bf16[16,2048]{1,0:T(8,128)(2,1)S(1)}, u32[]{:S(2)}, u32[]{:S(2)}) %collective-permute-start.12) | collective-permute-done | bytes 65568 | tf_op jit(solution)/shard_map/ppermute | solution.py:254
  37.5 1.7 %collective-permute-done.9.rest_2_ = bf16[16,2048]{1,0:T(8,128)(2,1)S(1)} collective-permute-done((bf16[16,2048]{1,0:T(8,128)(2,1)S(1)}, bf16[16,2048]{1,0:T(8,128)(2,1)S(1)}, u32[]{:S(2)}, u32[]{:S(2)}) %collective-permute-start.9) | collective-permute-done | bytes 65568 | tf_op jit(solution)/shard_map/ppermute | solution.py:254
  39.3 3.3 %down.1 = (f32[16,2048]{1,0:T(8,128)S(1)}, bf16[16,2048]{1,0:T(8,128)(2,1)S(1)}, bf16[16,2048]{1,0:T(8,128)(2,1)S(1)}, bf16[16,2048]{1,0:T(8,128)(2,1)S(1)}) custom-call(s32[16]{0:T(128)S(1)} %bitcast.17, s32[16,1,24]{2,1,0:T(1,128)S(1)} %copy-done.3, s32[20]{0:T(128)S(1)} %get-tuple-element.26.table_ref, ...), custom_call_target="tpu_custom_call" | custom-call | flops 805306368 | bytes 12582912 | tf_op jit(solution)/shard_map/down/pallas_call | solution.py:135
  42.6 4.1 %collective-permute-start.13 = (bf16[16,2048]{1,0:T(8,128)(2,1)S(1)}, bf16[16,2048]{1,0:T(8,128)(2,1)S(1)}, u32[]{:S(2)}, u32[]{:S(2)}) collective-permute-start(bf16[16,2048]{1,0:T(8,128)(2,1)S(1)} %get-tuple-element.42), channel_id=1, source_target_pairs={{0,2},{1,3},{2,0},{3,1},{4,6},{5,7},{6,4},{7,5},{8,10},{9,11},{10,... | collective-permute-start | bytes 196616 | tf_op jit(solution)/shard_map/ppermute | solution.py:203
  46.9 2.1 %collective-permute-done.13.rest_0_ = bf16[16,2048]{1,0:T(8,128)(2,1)S(1)} collective-permute-done((bf16[16,2048]{1,0:T(8,128)(2,1)S(1)}, bf16[16,2048]{1,0:T(8,128)(2,1)S(1)}, u32[]{:S(2)}, u32[]{:S(2)}) %collective-permute-start.13) | collective-permute-done | bytes 65568 | tf_op jit(solution)/shard_map/ppermute | solution.py:203
  49.0 1.4 %collective-permute-done.15.rest_2_ = bf16[16,2048]{1,0:T(8,128)(2,1)S(1)} collective-permute-done((bf16[16,2048]{1,0:T(8,128)(2,1)S(1)}, bf16[16,2048]{1,0:T(8,128)(2,1)S(1)}, u32[]{:S(2)}, u32[]{:S(2)}) %collective-permute-start.15) | collective-permute-done | bytes 65568 | tf_op jit(solution)/shard_map/ppermute | solution.py:203
  50.5 0.7 %last_sum.1 = bf16[16,2048]{1,0:T(8,128)(2,1)} custom-call(f32[16,2048]{1,0:T(8,128)S(1)} %get-tuple-element.41.own_ref, bf16[16,2048]{1,0:T(8,128)(2,1)S(1)} %collective-permute-done.13.rest_0_, bf16[16,2048]{1,0:T(8,128)(2,1)S(1)} %collective-permute-done.14.rest_1_, bf16[16,2048]{1,0:T(8,128)(2,1)S(1)} %collective-permute-done.15.rest_2_), custom_call_target="tpu_custom_call" | custom-call | tf_op jit(solution)/shard_map/last_sum/pallas_call | solution.py:148
  (37 shorter events, 0.6 us)
Async XLA Ops:
  0.0 6.9 %copy-start.5 = (s32[16,1]{0,1:T(1,128)S(1)}, s32[16,1]{0,1:T(1,128)}, u32[]{:S(2)}) copy-start(s32[16,1]{0,1:T(1,128)} %param.13) | copy-start | bytes 196
  0.0 6.9 %copy-start.4 = (s32[32,1]{0,1:T(1,128)S(1)}, s32[32,1]{0,1:T(1,128)}, u32[]{:S(2)}) copy-start(s32[32,1]{0,1:T(1,128)} %param.10) | copy-start | bytes 388
  0.0 12.4 %copy-start.2 = (s32[32,1,12]{0,1,2:T(1,128)S(1)}, s32[32,1,12]{0,1,2:T(1,128)}, u32[]{:S(2)}) copy-start(s32[32,1,12]{0,1,2:T(1,128)} %param.9) | copy-start | bytes 4612
  0.0 12.4 %copy-start = (bf16[32,1,12,128,256]{4,3,2,1,0:T(8,128)(2,1)S(1)}, bf16[32,1,12,128,256]{4,3,2,1,0:T(8,128)(2,1)}, u32[]{:S(2)}) copy-start(bf16[32,1,12,128,256]{4,3,2,1,0:T(8,128)(2,1)} %param.8) | copy-start | bytes 75497472
  0.8 8.2 %collective-permute-start.2 = (bf16[16,2048]{1,0:T(8,128)(2,1)S(1)}, bf16[16,2048]{1,0:T(8,128)(2,1)S(1)}, u32[]{:S(2)}, u32[]{:S(2)}) collective-permute-start(bf16[16,2048]{1,0:T(8,128)(2,1)S(1)} %copy-done.1), channel_id=1, source_target_pairs={{0,12},{4,0},{8,4},{12,8},{1,13},{5,1},{9,5},{13,9},{2,14},{6,2},{... | collective-permute-start | bytes 196616 | tf_op jit(solution)/shard_map/ppermute | solution.py:226
  5.9 6.5 %collective-permute-start.1 = (bf16[16,2048]{1,0:T(8,128)(2,1)S(1)}, bf16[16,2048]{1,0:T(8,128)(2,1)S(1)}, u32[]{:S(2)}, u32[]{:S(2)}) collective-permute-start(bf16[16,2048]{1,0:T(8,128)(2,1)S(1)} %copy-done.1), channel_id=1, source_target_pairs={{0,8},{4,12},{8,0},{12,4},{1,9},{5,13},{9,1},{13,5},{2,10},{6,14},... | collective-permute-start | bytes 196616 | tf_op jit(solution)/shard_map/ppermute | solution.py:226
  5.9 6.5 %collective-permute-start = (bf16[16,2048]{1,0:T(8,128)(2,1)S(1)}, bf16[16,2048]{1,0:T(8,128)(2,1)S(1)}, u32[]{:S(2)}, u32[]{:S(2)}) collective-permute-start(bf16[16,2048]{1,0:T(8,128)(2,1)S(1)} %copy-done.1), channel_id=1, source_target_pairs={{0,4},{4,8},{8,12},{12,0},{1,5},{5,9},{9,13},{13,1},{2,6},{6,10},{... | collective-permute-start | bytes 196616 | tf_op jit(solution)/shard_map/ppermute | solution.py:226
  12.4 26.9 %slice-start = ((s8[12582912]{0:T(1024)(128)(4,1)}), s8[4194304]{0:T(1024)(128)(4,1)S(1)}, s32[]{:S(2)}) async-start(s8[12582912]{0:T(1024)(128)(4,1)} %bitcast.7), calls=%async_computation | async-start | bytes 8388608
  12.4 26.9 %slice-start.1 = ((s8[12582912]{0:T(1024)(128)(4,1)}), s8[4194304]{0:T(1024)(128)(4,1)S(1)}, s32[]{:S(2)}) async-start(s8[12582912]{0:T(1024)(128)(4,1)} %bitcast.7), calls=%async_computation.1 | async-start | bytes 8388608
  12.4 26.9 %copy-start.3 = (s32[16,1,24]{2,1,0:T(1,128)S(1)}, s32[16,1,24]{2,1,0:T(1,128)}, u32[]{:S(2)}) copy-start(s32[16,1,24]{2,1,0:T(1,128)} %lists_ref.1) | copy-start | bytes 4612
  15.6 3.4 %collective-permute-start.5 = (bf16[32,4096]{1,0:T(8,128)(2,1)S(1)}, bf16[32,4096]{1,0:T(8,128)(2,1)S(1)}, u32[]{:S(2)}, u32[]{:S(2)}) collective-permute-start(bf16[32,4096]{1,0:T(8,128)(2,1)S(1)} %get-tuple-element.36), channel_id=1, source_target_pairs={{0,1},{1,0},{2,3},{3,2},{4,5},{5,4},{6,7},{7,6},{8,9},{9,8},{10,11... | collective-permute-start | bytes 786440 | tf_op jit(solution)/shard_map/ppermute | solution.py:203
  15.6 23.7 %slice-start.2 = ((s8[12582912]{0:T(1024)(128)(4,1)}), s8[4194304]{0:T(1024)(128)(4,1)S(1)}, s32[]{:S(2)}) async-start(s8[12582912]{0:T(1024)(128)(4,1)} %bitcast.7), calls=%async_computation.2 | async-start | bytes 8388608
  18.4 2.0 %collective-permute-start.3 = (bf16[32,4096]{1,0:T(8,128)(2,1)S(1)}, bf16[32,4096]{1,0:T(8,128)(2,1)S(1)}, u32[]{:S(2)}, u32[]{:S(2)}) collective-permute-start(bf16[32,4096]{1,0:T(8,128)(2,1)S(1)} %get-tuple-element.32), channel_id=1, source_target_pairs={{0,1},{1,0},{2,3},{3,2},{4,5},{5,4},{6,7},{7,6},{8,9},{9,8},{10,11... | collective-permute-start | bytes 786440 | tf_op jit(solution)/shard_map/ppermute | solution.py:203
  19.0 6.4 %collective-permute-start.6 = (bf16[16,4096]{1,0:T(8,128)(2,1)S(1)}, bf16[16,4096]{1,0:T(8,128)(2,1)S(1)}, u32[]{:S(2)}, u32[]{:S(2)}) collective-permute-start(bf16[16,4096]{1,0:T(8,128)(2,1)S(1)} %get-tuple-element.38), channel_id=1, source_target_pairs={{0,2},{1,3},{2,0},{3,1},{4,6},{5,7},{6,4},{7,5},{8,10},{9,11},{10,... | collective-permute-start | bytes 393224 | tf_op jit(solution)/shard_map/ppermute | solution.py:203
  20.5 6.9 %collective-permute-start.4 = (bf16[16,4096]{1,0:T(8,128)(2,1)S(1)}, bf16[16,4096]{1,0:T(8,128)(2,1)S(1)}, u32[]{:S(2)}, u32[]{:S(2)}) collective-permute-start(bf16[16,4096]{1,0:T(8,128)(2,1)S(1)} %get-tuple-element.34), channel_id=1, source_target_pairs={{0,2},{1,3},{2,0},{3,1},{4,6},{5,7},{6,4},{7,5},{8,10},{9,11},{10,... | collective-permute-start | bytes 393224 | tf_op jit(solution)/shard_map/ppermute | solution.py:203
  25.4 9.6 %collective-permute-start.11 = (bf16[16,2048]{1,0:T(8,128)(2,1)S(1)}, bf16[16,2048]{1,0:T(8,128)(2,1)S(1)}, u32[]{:S(2)}, u32[]{:S(2)}) collective-permute-start(bf16[16,2048]{1,0:T(8,128)(2,1)S(1)} %swiglu.2.rest_0_), channel_id=1, source_target_pairs={{0,12},{1,0},{2,4},{3,8},{4,13},{5,1},{6,5},{7,9},{8,14},{9,2},{10... | collective-permute-start | bytes 196616 | tf_op jit(solution)/shard_map/ppermute | solution.py:254
  27.4 11.8 %collective-permute-start.10 = (bf16[16,4096]{1,0:T(8,128)(2,1)S(1)}, bf16[16,4096]{1,0:T(8,128)(2,1)S(1)}, u32[]{:S(2)}, u32[]{:S(2)}) collective-permute-start(bf16[16,4096]{1,0:T(8,128)(2,1)S(1)} %get-tuple-element.39), channel_id=1, source_target_pairs={{0,8},{1,12},{2,0},{3,4},{4,9},{5,13},{6,1},{7,5},{8,10},{9,14},{1... | collective-permute-start | bytes 393224 | tf_op jit(solution)/shard_map/ppermute | solution.py:254
  29.3 10.0 %collective-permute-start.7 = (bf16[16,4096]{1,0:T(8,128)(2,1)S(1)}, bf16[16,4096]{1,0:T(8,128)(2,1)S(1)}, u32[]{:S(2)}, u32[]{:S(2)}) collective-permute-start(bf16[16,4096]{1,0:T(8,128)(2,1)S(1)} %get-tuple-element.39), channel_id=1, source_target_pairs={{0,0},{1,4},{2,8},{3,12},{4,1},{5,5},{6,9},{7,13},{8,2},{9,6},{10,... | collective-permute-start | bytes 393224 | tf_op jit(solution)/shard_map/ppermute | solution.py:254
  30.0 5.7 %collective-permute-start.8 = (bf16[16,2048]{1,0:T(8,128)(2,1)S(1)}, bf16[16,2048]{1,0:T(8,128)(2,1)S(1)}, u32[]{:S(2)}, u32[]{:S(2)}) collective-permute-start(bf16[16,2048]{1,0:T(8,128)(2,1)S(1)} %swiglu.2.rest_0_), channel_id=1, source_target_pairs={{0,4},{1,8},{2,12},{3,0},{4,5},{5,9},{6,13},{7,1},{8,6},{9,10},{10... | collective-permute-start | bytes 196616 | tf_op jit(solution)/shard_map/ppermute | solution.py:254
  33.0 4.5 %collective-permute-start.12 = (bf16[16,2048]{1,0:T(8,128)(2,1)S(1)}, bf16[16,2048]{1,0:T(8,128)(2,1)S(1)}, u32[]{:S(2)}, u32[]{:S(2)}) collective-permute-start(bf16[16,2048]{1,0:T(8,128)(2,1)S(1)} %get-tuple-element.40), channel_id=1, source_target_pairs={{0,12},{1,0},{2,4},{3,8},{4,13},{5,1},{6,5},{7,9},{8,14},{9,2},{10... | collective-permute-start | bytes 196616 | tf_op jit(solution)/shard_map/ppermute | solution.py:254
  35.1 4.2 %collective-permute-start.9 = (bf16[16,2048]{1,0:T(8,128)(2,1)S(1)}, bf16[16,2048]{1,0:T(8,128)(2,1)S(1)}, u32[]{:S(2)}, u32[]{:S(2)}) collective-permute-start(bf16[16,2048]{1,0:T(8,128)(2,1)S(1)} %get-tuple-element.40), channel_id=1, source_target_pairs={{0,4},{1,8},{2,12},{3,0},{4,5},{5,9},{6,13},{7,1},{8,6},{9,10},{10... | collective-permute-start | bytes 196616 | tf_op jit(solution)/shard_map/ppermute | solution.py:254
  42.6 6.4 %collective-permute-start.13 = (bf16[16,2048]{1,0:T(8,128)(2,1)S(1)}, bf16[16,2048]{1,0:T(8,128)(2,1)S(1)}, u32[]{:S(2)}, u32[]{:S(2)}) collective-permute-start(bf16[16,2048]{1,0:T(8,128)(2,1)S(1)} %get-tuple-element.42), channel_id=1, source_target_pairs={{0,2},{1,3},{2,0},{3,1},{4,6},{5,7},{6,4},{7,5},{8,10},{9,11},{10,... | collective-permute-start | bytes 196616 | tf_op jit(solution)/shard_map/ppermute | solution.py:203
  46.7 2.3 %collective-permute-start.14 = (bf16[16,2048]{1,0:T(8,128)(2,1)S(1)}, bf16[16,2048]{1,0:T(8,128)(2,1)S(1)}, u32[]{:S(2)}, u32[]{:S(2)}) collective-permute-start(bf16[16,2048]{1,0:T(8,128)(2,1)S(1)} %get-tuple-element.43), channel_id=1, source_target_pairs={{0,1},{1,0},{2,3},{3,2},{4,5},{5,4},{6,7},{7,6},{8,9},{9,8},{10,11... | collective-permute-start | bytes 196616 | tf_op jit(solution)/shard_map/ppermute | solution.py:203
  46.7 3.7 %collective-permute-start.15 = (bf16[16,2048]{1,0:T(8,128)(2,1)S(1)}, bf16[16,2048]{1,0:T(8,128)(2,1)S(1)}, u32[]{:S(2)}, u32[]{:S(2)}) collective-permute-start(bf16[16,2048]{1,0:T(8,128)(2,1)S(1)} %get-tuple-element.44), channel_id=1, source_target_pairs={{0,3},{1,2},{2,1},{3,0},{4,7},{5,6},{6,5},{7,4},{8,11},{9,10},{10,... | collective-permute-start | bytes 196616 | tf_op jit(solution)/shard_map/ppermute | solution.py:203
  (1 other events, 0.8 us)
